TPU v7x, 32 devices: a whole 2x2x4 slice. The times are simulated.
32 devices in a mesh: strip: 8 (over z, x), period: 4 (over y, core).
Axes of the slice: x: 2, y: 2, z: 4, core: 2. Of those that a mesh axis runs over, the one named last changes fastest.
Arguments:
- u_start: float32 [8, 16, 64, 128], P('strip', 'period'), may hold values from 0 to 0.02
- dual_prec: float32 [5, 8, 16, 64, 128], P(None, 'strip', 'period'), may hold values from 0 to 0.5
- dual_bound: float32 [8, 16, 64, 128], P('strip', 'period'), may hold values from 0 to 0.5
- dual_cap: float32 [16], P('period'), may hold values from 0 to 2
- capacity: float32 [16], P('period'), may hold values from 0.005 to 0.03
- block_value: float32 [8, 64, 128], P('strip'), may hold values from -6 to 6
- ton_class: int32 [8, 64, 128], P('strip'), may hold values from 0 to 7
- density: float32 [8], replicated, may hold values from 1 to 3
- slope_code: int32 [8, 128], P('strip'), may hold values from 0 to 15
- omega_start: float32 [1], replicated, may hold values from 0.5 to 2
Outputs:
- mined_share: float32 [8, 16, 64, 128], P('strip', 'period')
- arc_prices: float32 [5, 8, 16, 64, 128], P(None, 'strip', 'period')
- bound_prices: float32 [8, 16, 64, 128], P('strip', 'period')
- capacity_prices: float32 [16], P('period')
- primal_weight: float32 [1], replicated
All inputs are finite; a program needn't handle non-finite values.
Results may differ from a plain program's by a relative error of at most 0.0001.
Values sent between devices are 32-bit elements; how exact they have to be, the bound alone decides.
A program may use at most 64 MiB of HBM per device.

v0:
```python
import functools
import math

import jax
import jax.numpy as jnp
from jax import lax
from jax.experimental import pallas as pl
from jax.experimental.pallas import tpu as pltpu
from jax.sharding import PartitionSpec as P

OUTER = 2
INNER = 3
STEPS = OUTER * INNER
RATE = math.log(1.1) / 12.0
EPS = 1e-06
SLOPE = 11.0
MESH = pl.DeviceIdType.MESH


def kernel(
    NS, NPD, T, Z, Y, R,
    u_ref, prec_ref, bound_ref, cap_ref, capacity_ref, bv_ref, tc_ref, dens_ref, slope_ref, om_ref,
    u_out, prec_out, bound_out, cap_out, w_out,
    uf, uc, us, bf, bc, bs, fa, ca, sa, act, ton, tb, tl, cb, ex0,
    xs, xr, es, er, as_, ar, rs, rb, ps, pb, slr,
    praw, ti, to_sum, loc, ini_s, ini_r, xs_s, xs_r, e_s, e_r, a_s, a_r, r_s, r_r, p_s, p_r,
):
    me = lax.axis_index("strip")
    pe = lax.axis_index("period")
    total_rows = NS
    total_periods = NPD * T
    blocks_all = float(total_rows * Z * Y)
    root_blocks = math.sqrt(blocks_all)
    sends = []

    loads = (
        pltpu.make_async_copy(prec_ref.at[:, 0], praw, loc.at[0]),
        pltpu.make_async_copy(bound_ref.at[0], bf, loc.at[1]),
        pltpu.make_async_copy(u_ref.at[0], uf, loc.at[2]),
    )
    for load in loads:
        load.start()
    barrier = pltpu.get_barrier_semaphore()
    for k in range(1, NS):
        pl.semaphore_signal(barrier, inc=1, device_id={"strip": lax.rem(me + k, NS)}, device_id_type=MESH)
    for k in range(1, NPD):
        pl.semaphore_signal(barrier, inc=1, device_id={"period": lax.rem(pe + k, NPD)}, device_id_type=MESH)

    has = (me < NS - 1, me > 0)
    gets = (me > 0, me < NS - 1)
    to = (me + 1, me - 1)

    def remote(src, dst, ss, rr, dev):
        return pltpu.make_async_remote_copy(
            src_ref=src, dst_ref=dst, send_sem=ss, recv_sem=rr, device_id=dev, device_id_type=MESH
        )

    def ini_copy(d, what):
        if what == 2:
            return remote(to_sum.at[d], ti.at[d], ini_s.at[d, 2], ini_r.at[d, 2], {"strip": to[d]})
        if what == 0:
            rest = pl.ds(1, T - 1)
            return remote(praw.at[1 + d, rest], fa.at[5 + d, rest], ini_s.at[d, 0], ini_r.at[d, 0], {"strip": to[d]})
        return remote(slope_ref, slr.at[d], ini_s.at[d, 1], ini_r.at[d, 1], {"strip": to[d]})

    def x_copy(d, part, s):
        lo, size = (1, T - 1) if part == 0 else (0, 1)
        return remote(
            xs.at[s, pl.ds(lo, size)], xr.at[d, s, pl.ds(lo, size)],
            xs_s.at[d, part, s], xs_r.at[d, part, s], {"strip": to[d]},
        )

    def e_copy(k, s):
        return remote(es.at[s], er.at[s, k - 1], e_s.at[s, k - 1], e_r.at[s, k - 1], {"period": pe + k})

    def a_copy(k, s):
        return remote(as_.at[s], ar.at[s, k - 1], a_s.at[s, k - 1], a_r.at[s, k - 1], {"period": pe - k})

    def r_copy(k, slot):
        return remote(
            rs.at[slot], rb.at[slot, me], r_s.at[slot, k - 1], r_r.at[slot, k - 1],
            {"strip": lax.rem(me + k, NS)},
        )

    def p_copy(k, slot):
        return remote(
            ps.at[slot], pb.at[slot, pe], p_s.at[slot, k - 1], p_r.at[slot, k - 1],
            {"period": lax.rem(pe + k, NPD)},
        )

    def start(cond, copy):
        def go():
            copy.start()
        if cond is None:
            go()
        else:
            pl.when(cond)(go)
        sends.append((cond, copy))

    def wait_recv(cond, copy):
        if cond is None:
            copy.wait_recv()
        else:
            pl.when(cond)(lambda: copy.wait_recv())

    def reduce_start(slot, value):
        rs[slot] = value
        rb[slot, me] = value
        for k in range(1, NS):
            start(None, r_copy(k, slot))

    def reduce_done(slot):
        for k in range(1, NS):
            wait_recv(None, r_copy(k, slot))
        total = rb[slot, 0]
        for k in range(1, NS):
            total = total + rb[slot, k]
        return total

    loads[0].wait()
    for d in range(2):
        total = praw[1 + d, 0]
        for t in range(1, T):
            total = total + praw[1 + d, t]
        to_sum[d] = total
    pl.semaphore_wait(barrier, NS + NPD - 2)
    for d in range(2):
        start(has[d], ini_copy(d, 1))
        start(has[d], ini_copy(d, 2))
    for d in range(2):
        start(has[d], ini_copy(d, 0))

    rows = lax.broadcasted_iota(jnp.int32, (R, Y), 0)
    lanes = lax.broadcasted_iota(jnp.int32, (R, Y), 1)

    def as_lanes(value):
        sums = jnp.sum(value, axis=1, keepdims=True)
        return jnp.sum(jnp.where(lanes == rows, sums, 0.0), axis=0, keepdims=True)

    def as_rows(line):
        return jnp.sum(jnp.where(lanes == rows, line, 0.0), axis=1, keepdims=True)

    def fold(v):
        return jnp.sum(v.reshape(Z // 8, 8, Y), axis=0)

    cls = tc_ref[0]
    tons = jnp.zeros((Z, Y), jnp.float32)
    for c in range(dens_ref.shape[0]):
        tons = jnp.where(cls == c, (1.0 + c) * dens_ref[c], tons)
    ton[...] = tons
    part = jnp.sum(tons, axis=0, keepdims=True)
    reduce_start(0, part)

    z_ids = lax.broadcasted_iota(jnp.int32, (Z, Y), 0)
    y_ids = lax.broadcasted_iota(jnp.int32, (Z, Y), 1)

    def mask_of(codes, k, inside):
        ok = z_ids >= 1
        if k > 0:
            ok = ok & (jnp.broadcast_to((codes >> (k - 1)) & 1, (Z, Y)) == 1)
        if k == 3:
            ok = ok & (y_ids < Y - 1)
        if k == 4:
            ok = ok & (y_ids >= 1)
        if inside is not None:
            ok = ok & (jnp.full((Z, Y), inside.astype(jnp.int32)) == 1)
        return ok.astype(jnp.float32)

    own = slope_ref[...]
    act[0] = mask_of(own, 0, None)
    act[1] = mask_of(own, 1, me < NS - 1)
    act[2] = mask_of(own, 2, me > 0)
    act[3] = mask_of(own, 3, None)
    act[4] = mask_of(own, 4, None)

    period = [(pe * T + t).astype(jnp.float32) for t in range(T)]
    pid = [jnp.full((1, Y), period[t]) for t in range(T)]
    disc = [jnp.exp(-RATE * pid[t]) for t in range(T)]
    tonr = ton[...] * (1.0 / root_blocks)
    for load in loads[1:]:
        load.wait()
    for t in range(T):
        tb[t] = 1.0 / (SLOPE * (total_periods - pid[t]) + tonr)
        for k in range(5):
            fa[k, t] = praw[k, t] * act[k]

    caps = jnp.zeros((R, Y), jnp.float32)
    climit = jnp.zeros((R, Y), jnp.float32)
    for t in range(T):
        caps = jnp.where(rows == t, cap_ref[t], caps)
        climit = jnp.where(rows == t, capacity_ref[t] * blocks_all, climit)
    w = jnp.full((1, Y), om_ref[0])

    for d in range(2):
        @pl.when(jnp.logical_not(gets[d]))
        def _():
            act[5 + d] = jnp.zeros((Z, Y), jnp.float32)
            ti[d] = jnp.zeros((Z, Y), jnp.float32)
            fa[5 + d] = jnp.zeros((T, Z, Y), jnp.float32)
            for s in range(STEPS):
                xr[d, s] = jnp.zeros((T, Z, Y), jnp.float32)

    def up_y(v):
        return pltpu.roll(v, 1, 1)

    def dn_y(v):
        return pltpu.roll(v, Y - 1, 1)

    def up_z(v):
        return pltpu.roll(v, 1, 0)

    def dn_z(v):
        return pltpu.roll(v, Z - 1, 0)

    def settle(first, cur, acc, at, j, new, old):
        if j == 0:
            cur[at] = new
            return new, None
        if j == 1:
            cur[at] = new
            acc[at] = old + new
            return new, None
        mean = (acc[at] + new) * (1.0 / INNER)
        diff = mean - first[at]
        first[at] = mean
        return mean, fold(diff * diff)

    def gradient_own(arcs, bounds):
        for t in range(T):
            p0, p3, p4 = arcs[0, t], arcs[3, t], arcs[4, t]
            back = p0 + (up_y(p3) + dn_y(p4))
            tl[t] = ((p0 + p3) + (p4 + bounds[t])) - dn_z(back)

    def gradient(s, arcs):
        tail = None
        for t in range(T - 1, -1, -1):
            g = (tl[t] + (arcs[1, t] + arcs[2, t])) - dn_z(arcs[5, t] + arcs[6, t])
            tail = g if tail is None else tail + g
            tl[t] = tail
        as_[s] = tail
        for k in range(1, NPD):
            start(pe >= k, a_copy(k, s))

    tail = None
    for t in range(T - 1, -1, -1):
        p = [fa[k, t] for k in range(5)]
        g = (((p[0] + p[1]) + (p[2] + p[3])) + p[4]) + bf[t]
        g = g - dn_z(p[0] + (up_y(p[3]) + dn_y(p[4])))
        tail = g if tail is None else tail + g
        tl[t] = tail
    for d in range(2):
        wait_recv(gets[d], ini_copy(d, 1))
        wait_recv(gets[d], ini_copy(d, 2))

        @pl.when(gets[d])
        def _():
            act[5 + d] = mask_of(slr[d], 1 + d, None)
    as_[0] = tl[0] - dn_z(ti[0] * act[5] + ti[1] * act[6])
    for k in range(1, NPD):
        start(pe >= k, a_copy(k, 0))
    for d in range(2):
        wait_recv(gets[d], ini_copy(d, 0))
        rest = ti[d]
        for t in range(1, T):
            plane = fa[5 + d, t]
            rest = rest - plane
            fa[5 + d, t] = plane * act[5 + d]
        fa[5 + d, 0] = rest * act[5 + d]
    tail = None
    for t in range(T - 1, -1, -1):
        back = fa[5, t] + fa[6, t]
        tail = back if tail is None else tail + back
        tl[t] = tl[t] - dn_z(tail)
    tons_all = jnp.sum(reduce_done(0), axis=1, keepdims=True)
    inv_tons = 1.0 / tons_all
    cap_first = cap_sum = None

    for s in range(STEPS):
        j = s % INNER
        u_src = uf if j == 0 else uc
        b_src = bf if j == 0 else bc
        p_src = fa if j == 0 else ca
        inv_w = 1.0 / w
        move_p = jnp.zeros((8, Y), jnp.float32)
        move_d = jnp.zeros((8, Y), jnp.float32)
        for k in range(1, NPD):
            @pl.when(pe + k < NPD)
            def _():
                a_copy(k, s).wait_recv()
                for t in range(T):
                    tl[t] = tl[t] + ar[s, k - 1]
        head = None
        row = jnp.zeros((R, Y), jnp.float32)
        for t in range(T):
            old = u_src[t]
            grad = tl[t] + (ton[...] * (1.0 / root_blocks)) * caps[t : t + 1, :]
            new = jnp.maximum(old - (tb[t] * inv_w) * (grad - bv_ref[0] * disc[t]), 0.0)
            ext = 2.0 * new - old
            _, moved = settle(uf, uc, us, t, j, new, old)
            if moved is not None:
                move_p = move_p + moved
            if t == 0:
                ex0[...] = ext
            else:
                xs[s, t] = ext
            head = ext if head is None else head + ext
            row = jnp.where(rows == t, jnp.sum(ton[...] * ext, axis=0, keepdims=True), row)
        es[s] = head
        for k in range(1, NPD):
            start(pe + k < NPD, e_copy(k, s))
        for d in range(2):
            start(has[d], x_copy(d, 0, s))
        for k in range(1, NPD):
            @pl.when(pe >= k)
            def _():
                e_copy(k, s).wait_recv()
                ex0[...] = ex0[...] + er[s, k - 1]
        xs[s, 0] = ex0[...]
        for d in range(2):
            start(has[d], x_copy(d, 1, s))
        reduce_start(1 + s, as_lanes(row))
        total = None
        for t in range(T):
            total = xs[s, t] if t == 0 else total + xs[s, t]
            cb[t] = total
        rate_b = [w / (pid[t] + 1.0) for t in range(T)]
        rate_p = [w / (2.0 * (pid[t] + 1.0)) for t in range(T)]

        def arc(k, t, diff, move):
            old = p_src[k, t]
            new = jnp.maximum(old + rate_p[t] * diff, 0.0) * act[k]
            _, moved = settle(fa, ca, sa, (k, t), j, new, old)
            if moved is not None and k < 5:
                move = move + moved
            return move

        for t in range(T):
            c = cb[t]
            old = b_src[t]
            new = jnp.maximum(old + rate_b[t] * (c - 1.0), 0.0)
            _, moved = settle(bf, bc, bs, t, j, new, old)
            if moved is not None:
                move_d = move_d + moved
            cz = up_z(c)
            move_d = arc(0, t, c - cz, move_d)
            move_d = arc(3, t, c - dn_y(cz), move_d)
            move_d = arc(4, t, c - up_y(cz), move_d)
        last = j == INNER - 1
        if s < STEPS - 1:
            gradient_own(fa if last else ca, bf if last else bc)
        for part in range(2):
            for d in range(2):
                wait_recv(gets[d], x_copy(d, part, s))
        total_m = total_p = None
        for t in range(T):
            total_m = xr[0, s, t] if t == 0 else total_m + xr[0, s, t]
            total_p = xr[1, s, t] if t == 0 else total_p + xr[1, s, t]
            c = cb[t]
            cz = up_z(c)
            move_d = arc(1, t, c - up_z(total_p), move_d)
            move_d = arc(2, t, c - up_z(total_m), move_d)
            if s < STEPS - 1:
                arc(5, t, total_m - cz, None)
                arc(6, t, total_p - cz, None)
        if s < STEPS - 1:
            gradient(s + 1, fa if last else ca)
        if last:
            cyc = s // INNER
            mp = jnp.sum(move_p, axis=0, keepdims=True)
            md = jnp.sum(move_d, axis=0, keepdims=True)
            reduce_start(1 + STEPS + cyc, as_lanes(jnp.where(rows == 0, mp, jnp.where(rows == 1, md, 0.0))))
        row_total = as_rows(reduce_done(1 + s))
        new_caps = jnp.maximum(caps + w * ((row_total - climit) * inv_tons), 0.0)
        new_caps = jnp.where(rows < T, new_caps, 0.0)
        if j == 0:
            cap_first = caps
            cap_sum = new_caps
        else:
            cap_sum = cap_sum + new_caps
        caps = new_caps
        if last:
            caps = cap_sum * (1.0 / INNER)
            cap_move = jnp.sum((caps - cap_first) ** 2, axis=0, keepdims=True)
            got = reduce_done(1 + STEPS + cyc)
            msg = got + jnp.where(lanes[0:1] == 1, cap_move, 0.0)
            ps[cyc] = msg
            pb[cyc, pe] = msg
            for k in range(1, NPD):
                start(None, p_copy(k, cyc))
            if s == STEPS - 1:
                for t in range(T):
                    u_out[0, t] = uf[t]
                    bound_out[0, t] = bf[t]
                    for k in range(5):
                        prec_out[k, 0, t] = fa[k, t]
                    cap_out[t] = caps[t, 0]
            for k in range(1, NPD):
                wait_recv(None, p_copy(k, cyc))
            tot = pb[cyc, 0]
            for k in range(1, NPD):
                tot = tot + pb[cyc, k]
            tot = as_rows(tot)
            moved = jnp.sqrt((tot[1:2, :] + EPS) / (tot[0:1, :] + EPS))
            w = jnp.sqrt(w * moved)
    w_out[0] = w[0, 0]
    for cond, copy in sends:
        if cond is None:
            copy.wait_send()
        else:
            pl.when(cond)(lambda copy=copy: copy.wait_send())


def solution(mesh):
    NS, NPD = mesh.shape["strip"], mesh.shape["period"]

    def per_device(u, prec, bound, cap, capacity, bv, tc, dens, slope, om):
        rows_here, T, Z, Y = u.shape
        assert rows_here == 1
        R = -(-T // 8) * 8
        f32 = jnp.float32
        vmem = pl.BlockSpec(memory_space=pltpu.VMEM)
        hbm = pl.BlockSpec(memory_space=pl.ANY)
        smem = pl.BlockSpec(memory_space=pltpu.SMEM)
        plane = lambda *n: pltpu.VMEM((*n, Z, Y), f32)
        dma = pltpu.SemaphoreType.DMA
        slots = 1 + STEPS + OUTER
        far = max(NPD - 1, 1)
        return pl.pallas_call(
            functools.partial(kernel, NS, NPD, T, Z, Y, R),
            out_shape=(
                pltpu.VMEM(u.shape, f32),
                pltpu.VMEM(prec.shape, f32),
                pltpu.VMEM(bound.shape, f32),
                jax.ShapeDtypeStruct(cap.shape, f32),
                jax.ShapeDtypeStruct((1,), f32),
            ),
            in_specs=[hbm, hbm, hbm, smem, smem, vmem, vmem, smem, vmem, smem],
            out_specs=(vmem, vmem, vmem, smem, smem),
            scratch_shapes=[
                plane(T), plane(T), plane(T), plane(T), plane(T), plane(T),
                plane(7, T), plane(7, T), plane(7, T), plane(7), plane(), plane(T), plane(T), plane(T), plane(),
                plane(STEPS, T), plane(2, STEPS, T), plane(STEPS), plane(STEPS, far),
                plane(STEPS), plane(STEPS, far),
                pltpu.VMEM((slots, 1, Y), f32), pltpu.VMEM((slots, NS, 1, Y), f32),
                pltpu.VMEM((OUTER, 1, Y), f32), pltpu.VMEM((OUTER, NPD, 1, Y), f32),
                pltpu.VMEM((2, 1, Y), jnp.int32),
                plane(5, T), plane(2), plane(2), dma((3,)),
                dma((2, 3)), dma((2, 3)), dma((2, 2, STEPS)), dma((2, 2, STEPS)),
                dma((STEPS, far)), dma((STEPS, far)), dma((STEPS, far)), dma((STEPS, far)),
                dma((slots, NS - 1)), dma((slots, NS - 1)), dma((OUTER, far)), dma((OUTER, far)),
            ],
            compiler_params=pltpu.CompilerParams(collective_id=0, has_side_effects=True),
        )(u, prec, bound, cap, capacity, bv, tc, dens, slope, om)

    in_specs = (
        P("strip", "period", None, None),
        P(None, "strip", "period", None, None),
        P("strip", "period", None, None),
        P("period"),
        P("period"),
        P("strip", None, None),
        P("strip", None, None),
        P(),
        P("strip", None),
        P(),
    )
    out_specs = (
        P("strip", "period", None, None),
        P(None, "strip", "period", None, None),
        P("strip", "period", None, None),
        P("period"),
        P(),
    )
    return jax.shard_map(
        per_device, mesh=mesh, in_specs=in_specs, out_specs=out_specs, check_vma=False
    )
```

profile of v0, /device:TPU:0, one launch (start us, length us, event | category | flops | bytes accessed | tf_op | source)
XLA Modules:
  0.0 91.7 jit_solution(4046019571566960362)
XLA Ops:
  1.3 86.0 %shard_map.137 = (f32[1,4,64,128]{3,2,1,0:T(8,128)S(1)}, f32[5,1,4,64,128]{4,3,2,1,0:T(8,128)S(1)}, f32[1,4,64,128]{3,2,1,0:T(8,128)S(1)}, f32[4]{0:T(128)}, f32[1]{0:T(128)}) custom-call(f32[1,4,64,128]{3,2,1,0:T(8,128)} %u_ref.1, f32[5,1,4,64,128]{4,3,2,1,0:T(8,128)} %prec_ref.1, f32[1,4,64,128]{3,2,1,0:T(8,128)} %bound_ref.1, f32[4]{0:T(128)} %cap_ref.1, ...), custom_call_target="tpu_custom_call" | custom-call | tf_op jit(solution)/shard_map/pallas_call | solution.py:428
  87.3 0.7 copy.20
  87.9 0.7 copy.22
  88.6 0.0 copy-start
  88.6 0.8 copy.21
  89.4 0.0 copy-done
  89.4 0.5 copy.24
Async XLA Ops:
  88.6 0.8 copy-start
where the time goes:
time: 91.9 us; the launch traced here: 91.7 us
  Pallas kernels  86 us (94%)
  between operations  3.05 us (3%)
  local copies, waits for them, and re-layouts  2.66 us (3%)
    pallas_call x1, Pallas kernels, per_device(): pl.pallas_call(functools.partial(kernel, NS, NPD, T, Z, Y, R), out_shape=...  86 us
    unnamed x6, local copies, waits for them, and re-layouts  2.66 us

commit v1 on v0

--- a/solution.py
+++ b/solution.py
@@ -15,6 +15,8 @@
 EPS = 1e-06
 SLOPE = 11.0
 MESH = pl.DeviceIdType.MESH
+ROWS = 8
+CHUNK = 8
 
 
 def kernel(
@@ -410,12 +412,633 @@
             pl.when(cond)(lambda copy=copy: copy.wait_send())
 
 
+def pair_kernel(
+    NS, NPD, T, Z, Y,
+    u_ref, prec_ref, bound_ref, cap_ref, capacity_ref, bv_ref, tc_ref, dens_ref, slope_ref, om_ref,
+    u_out, prec_out, bound_out, cap_out, w_out,
+    praw, hh, pu, pb, pp, hpr, nraw, hnr, bvb, tcb, slr,
+    fa, ca, sa, fn, cn, sn, fh, ch, sh, bf, bc, bs, uf, uc, us,
+    act, nact, hact, ton, tb, pr, tl, tt, rp, rh,
+    xs, xr, hs, ls, zh, zl, dh, dl, rs, rb,
+    loc, ini_s, ini_r, sl_s, sl_r, sm_s, sm_r, re_s, re_r,
+    x_s, x_r, z_s, z_r, d_s, d_r, r_s, r_r, o_s, o_r,
+):
+    me = lax.axis_index("strip")
+    pe = lax.axis_index("period")
+    pairs, NP, NQ = NS // 2, NPD * T, 2 * NPD
+    NT = NP // ROWS
+    ND = NS * NPD
+    a, h = me // 2, lax.rem(me, 2)
+    q = jnp.where(h == 0, pe, NQ - 1 - pe)
+    blocks_all = float(NS * Z * Y)
+    inv_root = 1.0 / math.sqrt(blocks_all)
+    sends = []
+
+    def rows_of(block):
+        return pl.ds(pl.multiple_of(ROWS * block, ROWS), ROWS)
+
+    def block_of(hh_, pp_):
+        return jnp.where(hh_ == 0, pp_, NQ - 1 - pp_)
+
+    def device_at(pair, block):
+        first = block < NPD
+        return {
+            "strip": 2 * pair + jnp.where(first, 0, 1),
+            "period": jnp.where(first, block, NQ - 1 - block),
+        }
+
+    def remote(src, dst, ss, rr, dev):
+        return pltpu.make_async_remote_copy(
+            src_ref=src, dst_ref=dst, send_sem=ss, recv_sem=rr, device_id=dev, device_id_type=MESH
+        )
+
+    def start(cond, copy):
+        if cond is None:
+            copy.start()
+        else:
+            pl.when(cond)(lambda: copy.start())
+        sends.append((cond, copy))
+
+    def wait_recv(cond, copy):
+        if cond is None:
+            copy.wait_recv()
+        else:
+            pl.when(cond)(lambda: copy.wait_recv())
+
+    mine = pl.ds(pe * T, T)
+    loads = (
+        pltpu.make_async_copy(prec_ref.at[:, 0], praw, loc.at[0]),
+        pltpu.make_async_copy(prec_ref.at[:, 0, :, rows_of(q)], pp.at[:, h, mine], loc.at[1]),
+        pltpu.make_async_copy(bound_ref.at[0, :, rows_of(q)], pb.at[h, mine], loc.at[2]),
+        pltpu.make_async_copy(u_ref.at[0, :, rows_of(q)], pu.at[h, mine], loc.at[3]),
+        pltpu.make_async_copy(bv_ref.at[0, rows_of(q)], bvb.at[h], loc.at[4]),
+        pltpu.make_async_copy(tc_ref.at[0, rows_of(q)], tcb.at[h], loc.at[5]),
+    )
+    for load in loads:
+        load.start()
+    barrier = pltpu.get_barrier_semaphore()
+    others = [divmod(k, NPD) for k in range(1, ND)]
+
+    def other(ks, kp):
+        return {"strip": lax.rem(me + ks, NS), "period": lax.rem(pe + kp, NPD)}
+
+    for ks, kp in others:
+        pl.semaphore_signal(barrier, inc=1, device_id=other(ks, kp), device_id_type=MESH)
+
+    mates = [divmod(k, NPD) for k in range(1, NQ)]
+
+    def mate(i):
+        kh, kp = mates[i]
+        return lax.rem(h + kh, 2), lax.rem(pe + kp, NPD)
+
+    def in_copy(i, what):
+        th, tp = mate(i)
+        rows = rows_of(block_of(th, tp))
+        dev = {"strip": 2 * a + th, "period": tp}
+        ss, rr = ini_s.at[i, what], ini_r.at[i, what]
+        if what == 0:
+            return remote(prec_ref.at[pl.ds(1, 2), 0, :, rows], pp.at[pl.ds(1, 2), h, mine], ss, rr, dev)
+        if what == 1:
+            return remote(hh.at[block_of(th, tp)], hpr.at[pe, h], ss, rr, dev)
+        if what == 2:
+            return remote(prec_ref.at[0, 0, :, rows], pp.at[0, h, mine], ss, rr, dev)
+        if what == 3:
+            return remote(prec_ref.at[pl.ds(3, 2), 0, :, rows], pp.at[pl.ds(3, 2), h, mine], ss, rr, dev)
+        if what == 4:
+            return remote(bound_ref.at[0, :, rows], pb.at[h, mine], ss, rr, dev)
+        return remote(u_ref.at[0, :, rows], pu.at[h, mine], ss, rr, dev)
+
+    def partner_copy(what):
+        rows = rows_of(block_of(1 - h, pe))
+        dev = {"strip": 2 * a + 1 - h, "period": pe}
+        if what == 0:
+            return remote(tc_ref.at[0, rows], tcb.at[h], sm_s.at[0], sm_r.at[0], dev)
+        return remote(bv_ref.at[0, rows], bvb.at[h], sm_s.at[1], sm_r.at[1], dev)
+
+    has = (a > 0, a < pairs - 1)
+
+    def slope_copy(what):
+        if what == 0:
+            return remote(slope_ref, slr.at[1 + h], sl_s.at[0], sl_r.at[0], {"strip": 2 * a + 1 - h, "period": pe})
+        away = jnp.where(h == 0, a - 1, a + 1)
+        return remote(
+            slope_ref, slr.at[3 * (1 - h)], sl_s.at[what], sl_r.at[2 - h],
+            {"strip": 2 * away + what - 1, "period": pe},
+        )
+
+    def slope_wait(d):
+        return remote(slope_ref, slr.at[3 * d], sl_s.at[1], sl_r.at[1 + d], {"strip": lax.rem(me + 1, NS), "period": pe})
+
+    has_away = jnp.where(h == 0, a - 1, pairs - 2 - a) >= 0
+
+    def relay_copy(d, what):
+        dev = device_at(a - 1 if d == 0 else a + 1, q)
+        k, hs_ = (2, 0) if d == 0 else (1, 1)
+        ss, rr = re_s.at[d, what], re_r.at[d, what]
+        if what == 0:
+            return remote(pp.at[k, hs_], nraw.at[1 - d], ss, rr, dev)
+        return remote(hpr.at[:, hs_, k], hnr.at[1 - d], ss, rr, dev)
+
+    def reduce_copy(i, slot):
+        return remote(rs.at[slot], rb.at[slot, me * NPD + pe], r_s.at[slot, i], r_r.at[slot, i], other(*others[i]))
+
+    def reduce_start(slot, value):
+        rs[slot] = value
+        rb[slot, me * NPD + pe] = value
+        for i in range(ND - 1):
+            start(None, reduce_copy(i, slot))
+
+    def reduce_done(slot):
+        for i in range(ND - 1):
+            wait_recv(None, reduce_copy(i, slot))
+        parts = [rb[slot, i] for i in range(ND)]
+        while len(parts) > 1:
+            parts = [parts[i] + parts[i + 1] if i + 1 < len(parts) else parts[i] for i in range(0, len(parts), 2)]
+        return parts[0]
+
+    def x_copy(d, s):
+        dev = device_at(a - 1 if d == 0 else a + 1, q)
+        return remote(xs.at[s, d], xr.at[s, 1 - d], x_s.at[s, d], x_r.at[s, 1 - d], dev)
+
+    def z_copy(d, s):
+        if d == 0:
+            return remote(ls.at[s], zl.at[s], z_s.at[s, 0], z_r.at[s, 0], device_at(a, q - 1))
+        return remote(hs.at[s], zh.at[s], z_s.at[s, 1], z_r.at[s, 1], device_at(a, q + 1))
+
+    def d_copy(d, e, s):
+        dev = device_at(a - 1 if d == 0 else a + 1, q - 1 if e == 0 else q + 1)
+        src, dst = (ls, dl) if e == 0 else (hs, dh)
+        return remote(src.at[s, d], dst.at[s, 1 - d], d_s.at[s, d, e], d_r.at[s, 1 - d, e], dev)
+
+    def out_copy(i, what):
+        th, tp = mate(i)
+        dev = {"strip": 2 * a + th, "period": tp}
+        part = pl.ds(tp * T, T)
+        ss, rr = o_s.at[i, what], o_r.at[i, what]
+        rows = rows_of(q)
+        if what == 5:
+            return remote(uf.at[th, part], u_out.at[0, :, rows], ss, rr, dev)
+        if what == 6:
+            return remote(bf.at[th, part], bound_out.at[0, :, rows], ss, rr, dev)
+        return remote(fa.at[what, th, part], prec_out.at[what, 0, :, rows], ss, rr, dev)
+
+    up = (q > 0, q < NQ - 1)
+
+    for d in range(2):
+        @pl.when(jnp.logical_not(has[d]))
+        def _():
+            for s in range(STEPS):
+                xr[s, d] = jnp.zeros((NP, ROWS, Y), jnp.float32)
+            nraw[d] = jnp.zeros((NP, ROWS, Y), jnp.float32)
+            hnr[d] = jnp.zeros((NPD, T, Y), jnp.float32)
+            slr[3 * d] = jnp.zeros((1, Y), jnp.int32)
+        for e in range(2):
+            buf = (dh, dl)[e]
+
+            @pl.when(jnp.logical_not(has[d] & up[e]))
+            def _():
+                for s in range(STEPS):
+                    buf[s, d] = jnp.zeros((NT, ROWS, Y), jnp.float32)
+    for e in range(2):
+        buf = (zh, zl)[e]
+
+        @pl.when(jnp.logical_not(up[e]))
+        def _():
+            for s in range(STEPS):
+                buf[s] = jnp.zeros((2, NT, ROWS, Y), jnp.float32)
+
+    lanes1 = lax.broadcasted_iota(jnp.int32, (1, Y), 1)
+    rows = lax.broadcasted_iota(jnp.int32, (NP, Y), 0)
+    lanes = lax.broadcasted_iota(jnp.int32, (NP, Y), 1)
+
+    def tons_of(cls):
+        tons = jnp.zeros(cls.shape, jnp.float32)
+        for c in range(dens_ref.shape[0]):
+            tons = jnp.where(cls == c, (1.0 + c) * dens_ref[c], tons)
+        return tons
+
+    def as_lanes(value):
+        sums = jnp.sum(value, axis=1, keepdims=True)
+        return jnp.sum(jnp.where(lanes == rows, sums, 0.0), axis=0, keepdims=True)
+
+    def as_rows(line, at=0):
+        return jnp.broadcast_to(jnp.sum(jnp.where(lanes == rows + at, line, 0.0), axis=1, keepdims=True), (NP, Y))
+
+    slr[1 + h] = slope_ref[...]
+    loads[0].wait()
+    for b in range(NQ):
+        if b + 1 < NQ:
+            for k in range(5):
+                for t in range(T):
+                    hh[b, k, pl.ds(t, 1)] = praw[k, t, pl.ds(ROWS * (b + 1), 1)]
+        else:
+            hh[b] = jnp.zeros((5, T, Y), jnp.float32)
+    hpr[pe, h] = hh[q]
+    deep = Z // NPD
+    strip_part = tons_of(tc_ref[0, pl.ds(pl.multiple_of(pe * deep, ROWS), deep)])
+    strip_part = jnp.sum(jnp.sum(strip_part, axis=0, keepdims=True), axis=1, keepdims=True)
+    line = jnp.where(lanes1 == 2 * NP, strip_part, 0.0)
+    lead = jnp.where(me == 0, 1.0, 0.0)
+    for t in range(T):
+        line = jnp.where(lanes1 == pe * T + t, cap_ref[t] * lead, line)
+        line = jnp.where(lanes1 == NP + pe * T + t, capacity_ref[t] * lead, line)
+
+    pl.semaphore_wait(barrier, ND - 1)
+    for i in range(NQ - 1):
+        start(None, in_copy(i, 0))
+    for i in range(NQ - 1):
+        start(None, in_copy(i, 1))
+    start(None, slope_copy(0))
+    for what in (1, 2):
+        start(has_away, slope_copy(what))
+    start(None, partner_copy(0))
+    start(None, partner_copy(1))
+    reduce_start(0, line)
+    for what in range(2, 6):
+        for i in range(NQ - 1):
+            start(None, in_copy(i, what))
+
+    z_ids = lax.broadcasted_iota(jnp.int32, (ROWS, Y), 0)
+    y_ids = lax.broadcasted_iota(jnp.int32, (ROWS, Y), 1)
+    low = z_ids == ROWS - 1
+
+    def mask_of(code, k, depth, inside):
+        ok = (depth >= 1) & (depth < Z)
+        if k > 0:
+            ok = ok & (jnp.broadcast_to((code >> (k - 1)) & 1, (ROWS, Y)) == 1)
+        if k == 3:
+            ok = ok & (y_ids < Y - 1)
+        if k == 4:
+            ok = ok & (y_ids >= 1)
+        if inside is not None:
+            ok = ok & (jnp.full((ROWS, Y), inside.astype(jnp.int32)) == 1)
+        return ok.astype(jnp.float32)
+
+    wait_recv(None, slope_copy(0))
+    here, below = z_ids + ROWS * q, jnp.full((ROWS, Y), ROWS * (q + 1))
+    for hh_ in range(2):
+        code = slr[1 + hh_]
+        for k in range(5):
+            inside = None
+            if k == 1 and hh_ == 1:
+                inside = has[1]
+            if k == 2 and hh_ == 0:
+                inside = has[0]
+            act[k, hh_] = mask_of(code, k, here, inside)
+            hact[k, hh_] = mask_of(code, k, below, inside)
+    for d in range(2):
+        wait_recv(has[d], slope_wait(d))
+        nact[d] = mask_of(slr[3 * d], 1 + d, here + 1, has[d])
+
+    wait_recv(None, partner_copy(0))
+    wait_recv(None, partner_copy(1))
+    loads[4].wait()
+    loads[5].wait()
+    for hh_ in range(2):
+        tons = tons_of(tcb[hh_])
+        ton[hh_] = tons
+        for t in range(NP):
+            tb[hh_, t] = 1.0 / (SLOPE * (NP - t) + tons * inv_root)
+            pr[hh_, t] = bvb[hh_] * math.exp(-RATE * t)
+
+    t_plane = lax.broadcasted_iota(jnp.int32, (NP, ROWS, Y), 0).astype(jnp.float32)
+    t_rows = (
+        lax.broadcasted_iota(jnp.int32, (NT, ROWS, Y), 0) * ROWS + lax.broadcasted_iota(jnp.int32, (NT, ROWS, Y), 1)
+    ).astype(jnp.float32)
+
+    w = jnp.full((1, Y), om_ref[0])
+
+    def set_rates(w):
+        rp[...] = w[None] / (2.0 * (t_plane + 1.0))
+        rh[...] = w[None] / (2.0 * (t_rows + 1.0))
+
+    set_rates(w)
+
+    loads[1].wait()
+    for i in range(NQ - 1):
+        wait_recv(None, in_copy(i, 0))
+    for d in range(2):
+        start(has[d], relay_copy(d, 0))
+    for i in range(NQ - 1):
+        wait_recv(None, in_copy(i, 1))
+    for d in range(2):
+        start(has[d], relay_copy(d, 1))
+
+    chunks = [(lo, min(CHUNK, NP - lo)) for lo in range(0, NP, CHUNK)]
+
+    def roll(v, by, axis):
+        return pltpu.roll(v, by % v.shape[axis], axis)
+
+    def up_y(v):
+        return roll(v, 1, v.ndim - 1)
+
+    def dn_y(v):
+        return roll(v, -1, v.ndim - 1)
+
+    def lines(ref, lo, size, *at):
+        picked = [ref[(*at, t // ROWS, pl.ds(t % ROWS, 1))] for t in range(lo, lo + size)]
+        return jnp.stack([jnp.broadcast_to(p, (ROWS, Y)) for p in picked])
+
+    def from_above(v, line):
+        return jnp.where(lax.broadcasted_iota(jnp.int32, v.shape, 1) == 0, line, roll(v, 1, 1))
+
+    def from_below(v, line):
+        return jnp.where(lax.broadcasted_iota(jnp.int32, v.shape, 1) == ROWS - 1, line, roll(v, -1, 1))
+
+    def mask_arcs(ks):
+        for k in ks:
+            for hh_ in range(2):
+                fa[k, hh_] = pp[k, hh_] * act[k, hh_][None]
+
+    mask_arcs((1, 2))
+    for i in range(NQ - 1):
+        wait_recv(None, in_copy(i, 2))
+    mask_arcs((0,))
+    for i in range(NQ - 1):
+        wait_recv(None, in_copy(i, 3))
+    mask_arcs((3, 4))
+    for k in range(5):
+        for hh_ in range(2):
+            for p in range(NPD):
+                for t in range(T):
+                    at = p * T + t
+                    fh[k, hh_, at // ROWS, pl.ds(at % ROWS, 1)] = hpr[p, hh_, k, pl.ds(t, 1)] * hact[k, hh_, 0:1]
+    for d in range(2):
+        wait_recv(has[d], relay_copy(1 - d, 0))
+        wait_recv(has[d], relay_copy(1 - d, 1))
+        for t in range(NP):
+            edge = jnp.broadcast_to(hnr[d, t // T, pl.ds(t % T, 1)], (ROWS, Y))
+            fn[d, t] = jnp.where(low, edge, roll(nraw[d, t], -1, 0)) * nact[d]
+    loads[2].wait()
+    for i in range(NQ - 1):
+        wait_recv(None, in_copy(i, 4))
+
+    def settle(first, cur, acc, at, j, new, old):
+        if j == 0:
+            cur[at] = new
+            return None
+        if j == 1:
+            cur[at] = new
+            acc[at] = old + new
+            return None
+        mean = (acc[at] + new) * (1.0 / INNER)
+        diff = mean - first[at]
+        first[at] = mean
+        return jnp.sum(diff * diff, axis=0)
+
+    def gradient(arcs, near, halo, bounds):
+        for hh_ in range(2):
+            k_in = 2 if hh_ == 0 else 1
+            edge = (halo[0, hh_] + halo[k_in, 1 - hh_]) + (up_y(halo[3, hh_]) + dn_y(halo[4, hh_]))
+            hs_tmp = edge
+            tail = None
+            for lo, size in reversed(chunks):
+                at = pl.ds(lo, size)
+                p0, p3, p4 = arcs[0, hh_, at], arcs[3, hh_, at], arcs[4, hh_, at]
+                back = (p0 + arcs[k_in, 1 - hh_, at]) + (up_y(p3) + dn_y(p4))
+                rows_below = jnp.stack([
+                    jnp.broadcast_to(hs_tmp[t // ROWS, t % ROWS : t % ROWS + 1], (ROWS, Y)) for t in range(lo, lo + size)
+                ])
+                g = ((p0 + p3) + (p4 + bounds[hh_, at])) + (arcs[1, hh_, at] + arcs[2, hh_, at])
+                g = g - (from_below(back, rows_below) + near[hh_, at])
+                for t in range(lo + size - 1, lo - 1, -1):
+                    tail = g[t - lo] if tail is None else tail + g[t - lo]
+                    tl[hh_, t] = tail
+
+    gradient(fa, fn, fh, pb)
+    loads[3].wait()
+    for i in range(NQ - 1):
+        wait_recv(None, in_copy(i, 5))
+    got = reduce_done(0)
+    caps = as_rows(got)
+    climit = as_rows(got, NP) * blocks_all
+    inv_tons = 1.0 / jnp.sum(jnp.where(lanes1 == 2 * NP, got, 0.0), axis=1, keepdims=True)
+    cap_first = cap_sum = None
+
+    for s in range(STEPS):
+        j = s % INNER
+        last, final = j == INNER - 1, s == STEPS - 1
+        u_src = (pu if s == 0 else uf) if j == 0 else uc
+        b_src = (pb if s == 0 else bf) if j == 0 else bc
+        p_src, n_src, h_src = (fa, fn, fh) if j == 0 else (ca, cn, ch)
+        u_first, b_first = (pu, pb) if s < INNER else (uf, bf)
+        inv_w = 1.0 / w
+        move_p = jnp.zeros((ROWS, Y), jnp.float32)
+        move_d = jnp.zeros((ROWS, Y), jnp.float32)
+        if j == 0:
+            for hh_ in range(2):
+                for t in range(NP):
+                    tau = tb[hh_, t] * inv_w
+                    tt[hh_, t] = tau * (ton[hh_] * inv_root)
+                    tl[hh_, t] = u_src[hh_, t] - tau * (tl[hh_, t] - pr[hh_, t])
+        row = jnp.zeros((NP, Y), jnp.float32)
+        heads = [None, None]
+        for t in range(NP):
+            mined = None
+            for hh_ in range(2):
+                old = u_src[hh_, t]
+                new = jnp.maximum(tl[hh_, t] - tt[hh_, t] * caps[t : t + 1, :], 0.0)
+                ext = 2.0 * new - old
+                if j == 0:
+                    uc[hh_, t] = new
+                elif j == 1:
+                    uc[hh_, t] = new
+                    us[hh_, t] = old + new
+                else:
+                    mean = (us[hh_, t] + new) * (1.0 / INNER)
+                    diff = mean - u_first[hh_, t]
+                    uf[hh_, t] = mean
+                    move_p = move_p + diff * diff
+                heads[hh_] = ext if t == 0 else heads[hh_] + ext
+                xs[s, hh_, t] = heads[hh_]
+                hs[s, hh_, t // ROWS, pl.ds(t % ROWS, 1)] = heads[hh_][ROWS - 1 : ROWS]
+                if not final:
+                    ls[s, hh_, t // ROWS, pl.ds(t % ROWS, 1)] = heads[hh_][0:1]
+                part = ton[hh_] * ext
+                mined = part if mined is None else mined + part
+            row = jnp.where(rows == t, jnp.sum(mined, axis=0, keepdims=True), row)
+        reduce_start(1 + s, as_lanes(row))
+        start(up[1], z_copy(1, s))
+        for d in range(2):
+            start(has[d], x_copy(d, s))
+        for d in range(2):
+            start(has[d] & up[1], d_copy(d, 1, s))
+        if not final:
+            start(up[0], z_copy(0, s))
+            for d in range(2):
+                start(has[d] & up[0], d_copy(d, 0, s))
+        if final:
+            for i in range(NQ - 1):
+                start(None, out_copy(i, 5))
+
+        def arc(k, hh_, at, diff, move):
+            old = p_src[k, hh_, at]
+            new = jnp.maximum(old + rp[at] * diff, 0.0) * act[k, hh_][None]
+            moved = settle(fa, ca, sa, (k, hh_, at), j, new, old)
+            return move if moved is None else move + moved
+
+        for hh_ in range(2):
+            for lo, size in chunks:
+                at = pl.ds(lo, size)
+                old = b_src[hh_, at]
+                new = jnp.maximum(old + 2.0 * rp[at] * (xs[s, hh_, at] - 1.0), 0.0)
+                if j == 0:
+                    bc[hh_, at] = new
+                elif j == 1:
+                    bc[hh_, at] = new
+                    bs[hh_, at] = old + new
+                else:
+                    mean = (bs[hh_, at] + new) * (1.0 / INNER)
+                    diff = mean - b_first[hh_, at]
+                    bf[hh_, at] = mean
+                    move_d = move_d + jnp.sum(diff * diff, axis=0)
+        if final:
+            for i in range(NQ - 1):
+                start(None, out_copy(i, 6))
+        wait_recv(up[0], z_copy(1, s))
+        for lo, size in chunks:
+            at = pl.ds(lo, size)
+            c = [xs[s, hh_, at] for hh_ in range(2)]
+            cz = [from_above(c[hh_], lines(zh, lo, size, s, hh_)) for hh_ in range(2)]
+            for hh_ in range(2):
+                move_d = arc(0, hh_, at, c[hh_] - cz[hh_], move_d)
+                move_d = arc(3, hh_, at, c[hh_] - dn_y(cz[hh_]), move_d)
+                move_d = arc(4, hh_, at, c[hh_] - up_y(cz[hh_]), move_d)
+            move_d = arc(1, 0, at, c[0] - cz[1], move_d)
+            move_d = arc(2, 1, at, c[1] - cz[0], move_d)
+        if final:
+            for i in range(NQ - 1):
+                start(None, out_copy(i, 0))
+        for d in range(2):
+            wait_recv(has[d], x_copy(1 - d, s))
+            wait_recv(has[d] & up[0], d_copy(1 - d, 1, s))
+        for lo, size in chunks:
+            at = pl.ds(lo, size)
+            for d in range(2):
+                cz = from_above(xr[s, d, at], lines(dh, lo, size, s, d))
+                move_d = arc(2 - d, d, at, xs[s, d, at] - cz, move_d)
+        if last:
+            cyc = s // INNER
+            mp = jnp.sum(move_p, axis=0, keepdims=True)
+            md = jnp.sum(move_d, axis=0, keepdims=True)
+            reduce_start(1 + STEPS + cyc, as_lanes(jnp.where(rows == 0, mp, jnp.where(rows == 1, md, 0.0))))
+        if final:
+            for what in range(1, 5):
+                for i in range(NQ - 1):
+                    start(None, out_copy(i, what))
+        else:
+            wait_recv(up[1], z_copy(0, s))
+            for d in range(2):
+                wait_recv(has[d] & up[1], d_copy(1 - d, 0, s))
+            for lo, size in chunks:
+                at = pl.ds(lo, size)
+                for d in range(2):
+                    old = n_src[d, at]
+                    diff = from_below(xr[s, d, at], lines(dl, lo, size, s, d)) - xs[s, d, at]
+                    new = jnp.maximum(old + rp[at] * diff, 0.0) * nact[d][None]
+                    settle(fn, cn, sn, (d, at), j, new, old)
+            for hh_ in range(2):
+                c, cz = zl[s, hh_], hs[s, hh_]
+                for k in (0, 3, 4, 1 + hh_):
+                    ahead = (cz, hs[s, 1 - hh_], hs[s, 1 - hh_], dn_y(cz), up_y(cz))[k]
+                    old = h_src[k, hh_]
+                    new = jnp.maximum(old + rh[...] * (c - ahead), 0.0) * hact[k, hh_][None]
+                    settle(fh, ch, sh, (k, hh_), j, new, old)
+            if last:
+                gradient(fa, fn, fh, bf)
+            else:
+                gradient(ca, cn, ch, bc)
+                for hh_ in range(2):
+                    for t in range(NP):
+                        tau = tb[hh_, t] * inv_w
+                        tl[hh_, t] = uc[hh_, t] - tau * (tl[hh_, t] - pr[hh_, t])
+        row_total = as_rows(reduce_done(1 + s))
+        new_caps = jnp.maximum(caps + w * ((row_total - climit) * inv_tons), 0.0)
+        if j == 0:
+            cap_first = caps
+            cap_sum = new_caps
+        else:
+            cap_sum = cap_sum + new_caps
+        caps = new_caps
+        if last:
+            caps = cap_sum * (1.0 / INNER)
+            cap_move = jnp.sum((caps - cap_first) ** 2, axis=0, keepdims=True)
+            if final:
+                for t in range(T):
+                    own = jnp.sum(jnp.where(rows == pe * T + t, caps, 0.0), axis=0, keepdims=True)
+                    cap_out[t] = own[0, 0]
+            tot = as_rows(reduce_done(1 + STEPS + cyc))
+            moved = jnp.sqrt((tot[1:2, :] + cap_move + EPS) / (tot[0:1, :] + EPS))
+            w = jnp.sqrt(w * moved)
+            if not final:
+                set_rates(w)
+    w_out[0] = w[0, 0]
+    u_out[0, :, rows_of(q)] = uf[h, mine]
+    bound_out[0, :, rows_of(q)] = bf[h, mine]
+    for k in range(5):
+        prec_out[k, 0, :, rows_of(q)] = fa[k, h, mine]
+    for what in range(7):
+        for i in range(NQ - 1):
+            wait_recv(None, out_copy(i, what))
+    for cond, copy in sends:
+        if cond is None:
+            copy.wait_send()
+        else:
+            pl.when(cond)(lambda copy=copy: copy.wait_send())
+
+
+def pair_call(NS, NPD, u, prec, bound, cap, capacity, bv, tc, dens, slope, om):
+    _, T, Z, Y = u.shape
+    f32 = jnp.float32
+    NP, NQ, ND = NPD * T, 2 * NPD, NS * NPD
+    NT = NP // ROWS
+    vmem = pl.BlockSpec(memory_space=pltpu.VMEM)
+    hbm = pl.BlockSpec(memory_space=pl.ANY)
+    smem = pl.BlockSpec(memory_space=pltpu.SMEM)
+    slots = 1 + STEPS + OUTER
+    V = lambda *shape: pltpu.VMEM((*shape, Y), f32)
+    whole = lambda *n: V(*n, NP, ROWS)
+    edge = lambda *n: V(*n, NT, ROWS)
+    dma = pltpu.SemaphoreType.DMA
+    return pl.pallas_call(
+        functools.partial(pair_kernel, NS, NPD, T, Z, Y),
+        out_shape=(
+            pltpu.VMEM(u.shape, f32),
+            pltpu.VMEM(prec.shape, f32),
+            pltpu.VMEM(bound.shape, f32),
+            jax.ShapeDtypeStruct(cap.shape, f32),
+            jax.ShapeDtypeStruct((1,), f32),
+        ),
+        in_specs=[hbm, hbm, hbm, smem, smem, vmem, vmem, smem, vmem, smem],
+        out_specs=(vmem, vmem, vmem, smem, smem),
+        scratch_shapes=[
+            V(5, T, Z), V(NQ, 5, T), whole(2), whole(2), whole(5, 2), V(NPD, 2, 5, T), whole(2), V(2, NPD, T),
+            V(2, ROWS), pltpu.VMEM((2, ROWS, Y), jnp.int32), pltpu.VMEM((4, 1, Y), jnp.int32),
+            whole(5, 2), whole(5, 2), whole(5, 2), whole(2), whole(2), whole(2),
+            edge(5, 2), edge(5, 2), edge(5, 2), whole(2), whole(2), whole(2), whole(2), whole(2), whole(2),
+            V(5, 2, ROWS), V(2, ROWS), V(5, 2, ROWS), V(2, ROWS), whole(2), whole(2), whole(2), whole(2),
+            whole(), edge(),
+            whole(STEPS, 2), whole(STEPS, 2), edge(STEPS, 2), edge(STEPS, 2), edge(STEPS, 2), edge(STEPS, 2),
+            edge(STEPS, 2), edge(STEPS, 2), V(slots, 1), V(slots, ND, 1),
+            dma((6,)), dma((NQ - 1, 6)), dma((NQ - 1, 6)), dma((3,)), dma((3,)), dma((2,)), dma((2,)),
+            dma((2, 2)), dma((2, 2)),
+            dma((STEPS, 2)), dma((STEPS, 2)), dma((STEPS, 2)), dma((STEPS, 2)),
+            dma((STEPS, 2, 2)), dma((STEPS, 2, 2)), dma((slots, ND - 1)), dma((slots, ND - 1)),
+            dma((NQ - 1, 7)), dma((NQ - 1, 7)),
+        ],
+        compiler_params=pltpu.CompilerParams(collective_id=1, has_side_effects=True),
+    )(u, prec, bound, cap, capacity, bv, tc, dens, slope, om)
+
+
 def solution(mesh):
     NS, NPD = mesh.shape["strip"], mesh.shape["period"]
 
     def per_device(u, prec, bound, cap, capacity, bv, tc, dens, slope, om):
         rows_here, T, Z, Y = u.shape
         assert rows_here == 1
+        NP = NPD * T
+        if NS % 2 == 0 and Z == 2 * NPD * ROWS and NP % ROWS == 0 and 2 * NP < Y:
+            return pair_call(NS, NPD, u, prec, bound, cap, capacity, bv, tc, dens, slope, om)
         R = -(-T // 8) * 8
         f32 = jnp.float32
         vmem = pl.BlockSpec(memory_space=pltpu.VMEM)

time: 91.9 us -> 76.1 us (0.83)
  Pallas kernels: 86 us -> 70.1 us
    pallas_call x1, Pallas kernels: 86 us -> 70.1 us  [pair_call(): pl.pallas_call(functools.partial(pair_kernel, NS, NPD, T, Z, Y), out_shap...]
where the time goes in v1:
time: 76.1 us; the launch traced here: 75.9 us
  Pallas kernels  70.1 us (92%)
  between operations  3.05 us (4%)
  local copies, waits for them, and re-layouts  2.66 us (3%)
    pallas_call x1, Pallas kernels, pair_call(): pl.pallas_call(functools.partial(pair_kernel, NS, NPD, T, Z, Y), out_shap...  70.1 us
    unnamed x6, local copies, waits for them, and re-layouts  2.66 us

profile of v1, /device:TPU:0, one launch (start us, length us, event | category | flops | bytes accessed | tf_op | source)
XLA Modules:
  0.0 75.9 jit_solution(6299017269211598407)
XLA Ops:
  1.3 70.1 %shard_map.137 = (f32[1,4,64,128]{3,2,1,0:T(8,128)S(1)}, f32[5,1,4,64,128]{4,3,2,1,0:T(8,128)S(1)}, f32[1,4,64,128]{3,2,1,0:T(8,128)S(1)}, f32[4]{0:T(128)}, f32[1]{0:T(128)}) custom-call(f32[1,4,64,128]{3,2,1,0:T(8,128)} %u_ref.1, f32[5,1,4,64,128]{4,3,2,1,0:T(8,128)} %prec_ref.1, f32[1,4,64,128]{3,2,1,0:T(8,128)} %bound_ref.1, f32[4]{0:T(128)} %cap_ref.1, ...), custom_call_target="tpu_custom_call" | custom-call | tf_op jit(solution)/shard_map/pallas_call | solution.py:1003
  71.4 0.7 copy.20
  72.1 0.7 copy.22
  72.7 0.0 copy-start
  72.7 0.8 %copy.21 = f32[5,1,4,64,128]{4,3,2,1,0:T(8,128)} copy(f32[5,1,4,64,128]{4,3,2,1,0:T(8,128)S(1)} %get-tuple-element.6) | data formatting | bytes 1310720
  73.6 0.0 copy-done
  73.6 0.5 copy.24
Async XLA Ops:
  72.7 0.8 %copy-start = (f32[4]{0:T(128)S(1)}, f32[4]{0:T(128)}, u32[]{:S(2)}) copy-start(f32[4]{0:T(128)} %get-tuple-element.18) | copy-start | bytes 52

commit v2 on v1

--- a/solution.py
+++ b/solution.py
@@ -466,13 +466,13 @@
             pl.when(cond)(lambda: copy.wait_recv())
 
     mine = pl.ds(pe * T, T)
+    unit = h * NPD + pe
+    peers = pl.ds(0, NQ - 1)
     loads = (
         pltpu.make_async_copy(prec_ref.at[:, 0], praw, loc.at[0]),
-        pltpu.make_async_copy(prec_ref.at[:, 0, :, rows_of(q)], pp.at[:, h, mine], loc.at[1]),
-        pltpu.make_async_copy(bound_ref.at[0, :, rows_of(q)], pb.at[h, mine], loc.at[2]),
-        pltpu.make_async_copy(u_ref.at[0, :, rows_of(q)], pu.at[h, mine], loc.at[3]),
-        pltpu.make_async_copy(bv_ref.at[0, rows_of(q)], bvb.at[h], loc.at[4]),
-        pltpu.make_async_copy(tc_ref.at[0, rows_of(q)], tcb.at[h], loc.at[5]),
+        pltpu.make_async_copy(prec_ref.at[:, 0, :, rows_of(q)], pp.at[:, unit], loc.at[1]),
+        pltpu.make_async_copy(bound_ref.at[0, :, rows_of(q)], pb.at[unit], loc.at[2]),
+        pltpu.make_async_copy(u_ref.at[0, :, rows_of(q)], pu.at[unit], loc.at[3]),
     )
     for load in loads:
         load.start()
@@ -491,22 +491,25 @@
         kh, kp = mates[i]
         return lax.rem(h + kh, 2), lax.rem(pe + kp, NPD)
 
+    def in_ends(what, rows, block, at):
+        if what == 1:
+            return hh.at[block], hpr.at[at]
+        if what == 4:
+            return bound_ref.at[0, :, rows], pb.at[at]
+        if what == 5:
+            return u_ref.at[0, :, rows], pu.at[at]
+        arcs = (pl.ds(1, 2), None, 0, pl.ds(3, 2))[what]
+        return prec_ref.at[arcs, 0, :, rows], pp.at[arcs, at]
+
     def in_copy(i, what):
         th, tp = mate(i)
-        rows = rows_of(block_of(th, tp))
-        dev = {"strip": 2 * a + th, "period": tp}
-        ss, rr = ini_s.at[i, what], ini_r.at[i, what]
-        if what == 0:
-            return remote(prec_ref.at[pl.ds(1, 2), 0, :, rows], pp.at[pl.ds(1, 2), h, mine], ss, rr, dev)
-        if what == 1:
-            return remote(hh.at[block_of(th, tp)], hpr.at[pe, h], ss, rr, dev)
-        if what == 2:
-            return remote(prec_ref.at[0, 0, :, rows], pp.at[0, h, mine], ss, rr, dev)
-        if what == 3:
-            return remote(prec_ref.at[pl.ds(3, 2), 0, :, rows], pp.at[pl.ds(3, 2), h, mine], ss, rr, dev)
-        if what == 4:
-            return remote(bound_ref.at[0, :, rows], pb.at[h, mine], ss, rr, dev)
-        return remote(u_ref.at[0, :, rows], pu.at[h, mine], ss, rr, dev)
+        block = block_of(th, tp)
+        src, dst = in_ends(what, rows_of(block), block, unit)
+        return remote(src, dst, ini_s.at[what], ini_r.at[what], {"strip": 2 * a + th, "period": tp})
+
+    def in_all(what):
+        dst = in_ends(what, rows_of(0), 0, peers)[1]
+        return remote(dst, dst, ini_s.at[what], ini_r.at[what], other(0, 1))
 
     def partner_copy(what):
         rows = rows_of(block_of(1 - h, pe))
@@ -536,21 +539,23 @@
         k, hs_ = (2, 0) if d == 0 else (1, 1)
         ss, rr = re_s.at[d, what], re_r.at[d, what]
         if what == 0:
-            return remote(pp.at[k, hs_], nraw.at[1 - d], ss, rr, dev)
-        return remote(hpr.at[:, hs_, k], hnr.at[1 - d], ss, rr, dev)
-
-    def reduce_copy(i, slot):
-        return remote(rs.at[slot], rb.at[slot, me * NPD + pe], r_s.at[slot, i], r_r.at[slot, i], other(*others[i]))
+            return remote(pp.at[k, pl.ds(hs_ * NPD, NPD)], nraw.at[1 - d], ss, rr, dev)
+        return remote(hpr.at[pl.ds(hs_ * NPD, NPD), k], hnr.at[1 - d], ss, rr, dev)
+
+    def reduce_sem(slot):
+        return r_r.at[slot % 2 if slot <= STEPS else 2]
 
     def reduce_start(slot, value):
         rs[slot] = value
         rb[slot, me * NPD + pe] = value
-        for i in range(ND - 1):
-            start(None, reduce_copy(i, slot))
+        for ks, kp in others:
+            remote(
+                rs.at[slot], rb.at[slot, me * NPD + pe], r_s.at[0], reduce_sem(slot), other(ks, kp)
+            ).start()
 
     def reduce_done(slot):
-        for i in range(ND - 1):
-            wait_recv(None, reduce_copy(i, slot))
+        rest = rb.at[slot, pl.ds(0, ND - 1)]
+        remote(rest, rest, r_s.at[0], reduce_sem(slot), other(0, 1)).wait_recv()
         parts = [rb[slot, i] for i in range(ND)]
         while len(parts) > 1:
             parts = [parts[i] + parts[i + 1] if i + 1 < len(parts) else parts[i] for i in range(0, len(parts), 2)]
@@ -558,29 +563,35 @@
 
     def x_copy(d, s):
         dev = device_at(a - 1 if d == 0 else a + 1, q)
-        return remote(xs.at[s, d], xr.at[s, 1 - d], x_s.at[s, d], x_r.at[s, 1 - d], dev)
+        return remote(xs.at[s, d], xr.at[s, 1 - d], x_s.at[d], x_r.at[s % 2, 1 - d], dev)
 
     def z_copy(d, s):
         if d == 0:
-            return remote(ls.at[s], zl.at[s], z_s.at[s, 0], z_r.at[s, 0], device_at(a, q - 1))
-        return remote(hs.at[s], zh.at[s], z_s.at[s, 1], z_r.at[s, 1], device_at(a, q + 1))
+            return remote(ls.at[s], zl.at[s], z_s.at[0], z_r.at[s % 2, 0], device_at(a, q - 1))
+        return remote(hs.at[s], zh.at[s], z_s.at[1], z_r.at[s % 2, 1], device_at(a, q + 1))
 
     def d_copy(d, e, s):
         dev = device_at(a - 1 if d == 0 else a + 1, q - 1 if e == 0 else q + 1)
         src, dst = (ls, dl) if e == 0 else (hs, dh)
-        return remote(src.at[s, d], dst.at[s, 1 - d], d_s.at[s, d, e], d_r.at[s, 1 - d, e], dev)
-
-    def out_copy(i, what):
-        th, tp = mate(i)
-        dev = {"strip": 2 * a + th, "period": tp}
-        part = pl.ds(tp * T, T)
-        ss, rr = o_s.at[i, what], o_r.at[i, what]
-        rows = rows_of(q)
-        if what == 5:
-            return remote(uf.at[th, part], u_out.at[0, :, rows], ss, rr, dev)
-        if what == 6:
-            return remote(bf.at[th, part], bound_out.at[0, :, rows], ss, rr, dev)
-        return remote(fa.at[what, th, part], prec_out.at[what, 0, :, rows], ss, rr, dev)
+        return remote(src.at[s, d], dst.at[s, 1 - d], d_s.at[d, e], d_r.at[s % 2, 1 - d, e], dev)
+
+    def out_ends(what, th, part, rows):
+        if what == 0:
+            return uf.at[th, part], u_out.at[0, :, rows]
+        if what == 1:
+            return bf.at[th, part], bound_out.at[0, :, rows]
+        arcs = (0, pl.ds(3, 2), pl.ds(1, 2))[what - 2]
+        return fa.at[arcs, th, part], prec_out.at[arcs, 0, :, rows]
+
+    def out_start(what):
+        for i in range(NQ - 1):
+            th, tp = mate(i)
+            src, dst = out_ends(what, th, pl.ds(tp * T, T), rows_of(q))
+            remote(src, dst, o_s.at[what], o_r.at[what], {"strip": 2 * a + th, "period": tp}).start()
+
+    def out_all(what):
+        dst = out_ends(what, 0, mine, pl.ds(0, ROWS * (NQ - 1)))[1]
+        return remote(dst, dst, o_s.at[what], o_r.at[what], other(0, 1))
 
     up = (q > 0, q < NQ - 1)
 
@@ -589,7 +600,7 @@
         def _():
             for s in range(STEPS):
                 xr[s, d] = jnp.zeros((NP, ROWS, Y), jnp.float32)
-            nraw[d] = jnp.zeros((NP, ROWS, Y), jnp.float32)
+            nraw[d] = jnp.zeros((NPD, T, ROWS, Y), jnp.float32)
             hnr[d] = jnp.zeros((NPD, T, Y), jnp.float32)
             slr[3 * d] = jnp.zeros((1, Y), jnp.int32)
         for e in range(2):
@@ -633,7 +644,9 @@
                     hh[b, k, pl.ds(t, 1)] = praw[k, t, pl.ds(ROWS * (b + 1), 1)]
         else:
             hh[b] = jnp.zeros((5, T, Y), jnp.float32)
-    hpr[pe, h] = hh[q]
+    hpr[unit] = hh[q]
+    bvb[h] = bv_ref[0, rows_of(q)]
+    tcb[h] = tc_ref[0, rows_of(q)]
     deep = Z // NPD
     strip_part = tons_of(tc_ref[0, pl.ds(pl.multiple_of(pe * deep, ROWS), deep)])
     strip_part = jnp.sum(jnp.sum(strip_part, axis=0, keepdims=True), axis=1, keepdims=True)
@@ -644,10 +657,9 @@
         line = jnp.where(lanes1 == NP + pe * T + t, capacity_ref[t] * lead, line)
 
     pl.semaphore_wait(barrier, ND - 1)
-    for i in range(NQ - 1):
-        start(None, in_copy(i, 0))
-    for i in range(NQ - 1):
-        start(None, in_copy(i, 1))
+    for what in range(2):
+        for i in range(NQ - 1):
+            in_copy(i, what).start()
     start(None, slope_copy(0))
     for what in (1, 2):
         start(has_away, slope_copy(what))
@@ -656,7 +668,7 @@
     reduce_start(0, line)
     for what in range(2, 6):
         for i in range(NQ - 1):
-            start(None, in_copy(i, what))
+            in_copy(i, what).start()
 
     z_ids = lax.broadcasted_iota(jnp.int32, (ROWS, Y), 0)
     y_ids = lax.broadcasted_iota(jnp.int32, (ROWS, Y), 1)
@@ -692,8 +704,6 @@
 
     wait_recv(None, partner_copy(0))
     wait_recv(None, partner_copy(1))
-    loads[4].wait()
-    loads[5].wait()
     for hh_ in range(2):
         tons = tons_of(tcb[hh_])
         ton[hh_] = tons
@@ -715,12 +725,10 @@
     set_rates(w)
 
     loads[1].wait()
-    for i in range(NQ - 1):
-        wait_recv(None, in_copy(i, 0))
+    in_all(0).wait_recv()
     for d in range(2):
         start(has[d], relay_copy(d, 0))
-    for i in range(NQ - 1):
-        wait_recv(None, in_copy(i, 1))
+    in_all(1).wait_recv()
     for d in range(2):
         start(has[d], relay_copy(d, 1))
 
@@ -745,33 +753,33 @@
     def from_below(v, line):
         return jnp.where(lax.broadcasted_iota(jnp.int32, v.shape, 1) == ROWS - 1, line, roll(v, -1, 1))
 
+    def landed(ref, hh_, *at):
+        return ref[(*at, pl.ds(hh_ * NPD, NPD))].reshape(NP, ROWS, Y)
+
     def mask_arcs(ks):
         for k in ks:
             for hh_ in range(2):
-                fa[k, hh_] = pp[k, hh_] * act[k, hh_][None]
+                fa[k, hh_] = landed(pp, hh_, k) * act[k, hh_][None]
 
     mask_arcs((1, 2))
-    for i in range(NQ - 1):
-        wait_recv(None, in_copy(i, 2))
+    in_all(2).wait_recv()
     mask_arcs((0,))
-    for i in range(NQ - 1):
-        wait_recv(None, in_copy(i, 3))
+    in_all(3).wait_recv()
     mask_arcs((3, 4))
     for k in range(5):
         for hh_ in range(2):
             for p in range(NPD):
                 for t in range(T):
                     at = p * T + t
-                    fh[k, hh_, at // ROWS, pl.ds(at % ROWS, 1)] = hpr[p, hh_, k, pl.ds(t, 1)] * hact[k, hh_, 0:1]
+                    fh[k, hh_, at // ROWS, pl.ds(at % ROWS, 1)] = hpr[hh_ * NPD + p, k, pl.ds(t, 1)] * hact[k, hh_, 0:1]
     for d in range(2):
         wait_recv(has[d], relay_copy(1 - d, 0))
         wait_recv(has[d], relay_copy(1 - d, 1))
         for t in range(NP):
             edge = jnp.broadcast_to(hnr[d, t // T, pl.ds(t % T, 1)], (ROWS, Y))
-            fn[d, t] = jnp.where(low, edge, roll(nraw[d, t], -1, 0)) * nact[d]
+            fn[d, t] = jnp.where(low, edge, roll(nraw[d, t // T, t % T], -1, 0)) * nact[d]
     loads[2].wait()
-    for i in range(NQ - 1):
-        wait_recv(None, in_copy(i, 4))
+    in_all(4).wait_recv()
 
     def settle(first, cur, acc, at, j, new, old):
         if j == 0:
@@ -805,10 +813,13 @@
                     tail = g[t - lo] if tail is None else tail + g[t - lo]
                     tl[hh_, t] = tail
 
-    gradient(fa, fn, fh, pb)
+    for hh_ in range(2):
+        bf[hh_] = landed(pb, hh_)
+    gradient(fa, fn, fh, bf)
     loads[3].wait()
-    for i in range(NQ - 1):
-        wait_recv(None, in_copy(i, 5))
+    in_all(5).wait_recv()
+    for hh_ in range(2):
+        uf[hh_] = landed(pu, hh_)
     got = reduce_done(0)
     caps = as_rows(got)
     climit = as_rows(got, NP) * blocks_all
@@ -818,10 +829,9 @@
     for s in range(STEPS):
         j = s % INNER
         last, final = j == INNER - 1, s == STEPS - 1
-        u_src = (pu if s == 0 else uf) if j == 0 else uc
-        b_src = (pb if s == 0 else bf) if j == 0 else bc
+        u_src = uf if j == 0 else uc
+        b_src = bf if j == 0 else bc
         p_src, n_src, h_src = (fa, fn, fh) if j == 0 else (ca, cn, ch)
-        u_first, b_first = (pu, pb) if s < INNER else (uf, bf)
         inv_w = 1.0 / w
         move_p = jnp.zeros((ROWS, Y), jnp.float32)
         move_d = jnp.zeros((ROWS, Y), jnp.float32)
@@ -846,7 +856,7 @@
                     us[hh_, t] = old + new
                 else:
                     mean = (us[hh_, t] + new) * (1.0 / INNER)
-                    diff = mean - u_first[hh_, t]
+                    diff = mean - uf[hh_, t]
                     uf[hh_, t] = mean
                     move_p = move_p + diff * diff
                 heads[hh_] = ext if t == 0 else heads[hh_] + ext
@@ -858,18 +868,17 @@
                 mined = part if mined is None else mined + part
             row = jnp.where(rows == t, jnp.sum(mined, axis=0, keepdims=True), row)
         reduce_start(1 + s, as_lanes(row))
-        start(up[1], z_copy(1, s))
+        pl.when(up[1])(z_copy(1, s).start)
         for d in range(2):
-            start(has[d], x_copy(d, s))
+            pl.when(has[d])(x_copy(d, s).start)
         for d in range(2):
-            start(has[d] & up[1], d_copy(d, 1, s))
+            pl.when(has[d] & up[1])(d_copy(d, 1, s).start)
         if not final:
-            start(up[0], z_copy(0, s))
+            pl.when(up[0])(z_copy(0, s).start)
             for d in range(2):
-                start(has[d] & up[0], d_copy(d, 0, s))
+                pl.when(has[d] & up[0])(d_copy(d, 0, s).start)
         if final:
-            for i in range(NQ - 1):
-                start(None, out_copy(i, 5))
+            out_start(0)
 
         def arc(k, hh_, at, diff, move):
             old = p_src[k, hh_, at]
@@ -889,12 +898,11 @@
                     bs[hh_, at] = old + new
                 else:
                     mean = (bs[hh_, at] + new) * (1.0 / INNER)
-                    diff = mean - b_first[hh_, at]
+                    diff = mean - bf[hh_, at]
                     bf[hh_, at] = mean
                     move_d = move_d + jnp.sum(diff * diff, axis=0)
         if final:
-            for i in range(NQ - 1):
-                start(None, out_copy(i, 6))
+            out_start(1)
         wait_recv(up[0], z_copy(1, s))
         for lo, size in chunks:
             at = pl.ds(lo, size)
@@ -907,8 +915,8 @@
             move_d = arc(1, 0, at, c[0] - cz[1], move_d)
             move_d = arc(2, 1, at, c[1] - cz[0], move_d)
         if final:
-            for i in range(NQ - 1):
-                start(None, out_copy(i, 0))
+            out_start(2)
+            out_start(3)
         for d in range(2):
             wait_recv(has[d], x_copy(1 - d, s))
             wait_recv(has[d] & up[0], d_copy(1 - d, 1, s))
@@ -923,9 +931,7 @@
             md = jnp.sum(move_d, axis=0, keepdims=True)
             reduce_start(1 + STEPS + cyc, as_lanes(jnp.where(rows == 0, mp, jnp.where(rows == 1, md, 0.0))))
         if final:
-            for what in range(1, 5):
-                for i in range(NQ - 1):
-                    start(None, out_copy(i, what))
+            out_start(4)
         else:
             wait_recv(up[1], z_copy(0, s))
             for d in range(2):
@@ -977,9 +983,25 @@
     bound_out[0, :, rows_of(q)] = bf[h, mine]
     for k in range(5):
         prec_out[k, 0, :, rows_of(q)] = fa[k, h, mine]
-    for what in range(7):
-        for i in range(NQ - 1):
-            wait_recv(None, out_copy(i, what))
+    for what in range(5):
+        out_all(what).wait_recv()
+    for what in range(5):
+        out_all(what).wait_send()
+    for what in range(6):
+        in_all(what).wait_send()
+    rest = rb.at[:, pl.ds(0, ND - 1)]
+    remote(rest, rest, r_s.at[0], r_r.at[0], other(0, 1)).wait_send()
+
+    def wait_sent(cond, ref, sem):
+        pl.when(cond)(lambda: remote(ref, ref, sem, sem, other(0, 1)).wait_send())
+
+    rows_down, rows_up = ls.at[pl.ds(0, STEPS - 1)], hs
+    wait_sent(up[0], rows_down, z_s.at[0])
+    wait_sent(up[1], rows_up, z_s.at[1])
+    for d in range(2):
+        wait_sent(has[d], xs.at[:, d], x_s.at[d])
+        wait_sent(has[d] & up[0], ls.at[pl.ds(0, STEPS - 1), d], d_s.at[d, 0])
+        wait_sent(has[d] & up[1], hs.at[:, d], d_s.at[d, 1])
     for cond, copy in sends:
         if cond is None:
             copy.wait_send()
@@ -997,6 +1019,7 @@
     smem = pl.BlockSpec(memory_space=pltpu.SMEM)
     slots = 1 + STEPS + OUTER
     V = lambda *shape: pltpu.VMEM((*shape, Y), f32)
+    unit = lambda *n: V(*n, NQ, T, ROWS)
     whole = lambda *n: V(*n, NP, ROWS)
     edge = lambda *n: V(*n, NT, ROWS)
     dma = pltpu.SemaphoreType.DMA
@@ -1012,7 +1035,7 @@
         in_specs=[hbm, hbm, hbm, smem, smem, vmem, vmem, smem, vmem, smem],
         out_specs=(vmem, vmem, vmem, smem, smem),
         scratch_shapes=[
-            V(5, T, Z), V(NQ, 5, T), whole(2), whole(2), whole(5, 2), V(NPD, 2, 5, T), whole(2), V(2, NPD, T),
+            V(5, T, Z), V(NQ, 5, T), unit(), unit(), unit(5), V(NQ, 5, T), V(2, NPD, T, ROWS), V(2, NPD, T),
             V(2, ROWS), pltpu.VMEM((2, ROWS, Y), jnp.int32), pltpu.VMEM((4, 1, Y), jnp.int32),
             whole(5, 2), whole(5, 2), whole(5, 2), whole(2), whole(2), whole(2),
             edge(5, 2), edge(5, 2), edge(5, 2), whole(2), whole(2), whole(2), whole(2), whole(2), whole(2),
@@ -1020,11 +1043,9 @@
             whole(), edge(),
             whole(STEPS, 2), whole(STEPS, 2), edge(STEPS, 2), edge(STEPS, 2), edge(STEPS, 2), edge(STEPS, 2),
             edge(STEPS, 2), edge(STEPS, 2), V(slots, 1), V(slots, ND, 1),
-            dma((6,)), dma((NQ - 1, 6)), dma((NQ - 1, 6)), dma((3,)), dma((3,)), dma((2,)), dma((2,)),
-            dma((2, 2)), dma((2, 2)),
-            dma((STEPS, 2)), dma((STEPS, 2)), dma((STEPS, 2)), dma((STEPS, 2)),
-            dma((STEPS, 2, 2)), dma((STEPS, 2, 2)), dma((slots, ND - 1)), dma((slots, ND - 1)),
-            dma((NQ - 1, 7)), dma((NQ - 1, 7)),
+            dma((4,)), dma((6,)), dma((6,)), dma((3,)), dma((3,)), dma((2,)), dma((2,)), dma((2, 2)), dma((2, 2)),
+            dma((2,)), dma((2, 2)), dma((2,)), dma((2, 2)), dma((2, 2)), dma((2, 2, 2)), dma((1,)), dma((3,)),
+            dma((5,)), dma((5,)),
         ],
         compiler_params=pltpu.CompilerParams(collective_id=1, has_side_effects=True),
     )(u, prec, bound, cap, capacity, bv, tc, dens, slope, om)

time: 76.1 us -> 68 us (0.89)
  Pallas kernels: 70.1 us -> 62.1 us
    pallas_call x1, Pallas kernels: 70.1 us -> 62.1 us  [pair_call(): pl.pallas_call(functools.partial(pair_kernel, NS, NPD, T, Z, Y), out_shap...]
where the time goes in v2:
time: 68 us; the launch traced here: 67.8 us
  Pallas kernels  62.1 us (91%)
  between operations  3.05 us (4%)
  local copies, waits for them, and re-layouts  2.66 us (4%)
    pallas_call x1, Pallas kernels, pair_call(): pl.pallas_call(functools.partial(pair_kernel, NS, NPD, T, Z, Y), out_shap...  62.1 us
    unnamed x6, local copies, waits for them, and re-layouts  2.66 us

profile of v2, /device:TPU:0, one launch (start us, length us, event | category | flops | bytes accessed | tf_op | source)
XLA Modules:
  0.0 67.8 jit_solution(8254135014847657041)
XLA Ops:
  1.3 62.1 %shard_map.137 = (f32[1,4,64,128]{3,2,1,0:T(8,128)S(1)}, f32[5,1,4,64,128]{4,3,2,1,0:T(8,128)S(1)}, f32[1,4,64,128]{3,2,1,0:T(8,128)S(1)}, f32[4]{0:T(128)}, f32[1]{0:T(128)}) custom-call(f32[1,4,64,128]{3,2,1,0:T(8,128)} %u_ref.1, f32[5,1,4,64,128]{4,3,2,1,0:T(8,128)} %prec_ref.1, f32[1,4,64,128]{3,2,1,0:T(8,128)} %bound_ref.1, f32[4]{0:T(128)} %cap_ref.1, ...), custom_call_target="tpu_custom_call" | custom-call | tf_op jit(solution)/shard_map/pallas_call | solution.py:1026
  63.4 0.7 copy.20
  64.0 0.7 copy.22
  64.7 0.0 copy-start
  64.7 0.8 %copy.21 = f32[5,1,4,64,128]{4,3,2,1,0:T(8,128)} copy(f32[5,1,4,64,128]{4,3,2,1,0:T(8,128)S(1)} %get-tuple-element.6) | data formatting | bytes 1310720
  65.5 0.0 copy-done
  65.5 0.5 copy.24
Async XLA Ops:
  64.7 0.8 %copy-start = (f32[4]{0:T(128)S(1)}, f32[4]{0:T(128)}, u32[]{:S(2)}) copy-start(f32[4]{0:T(128)} %get-tuple-element.18) | copy-start | bytes 52

commit v3 on v2

--- a/solution.py
+++ b/solution.py
@@ -415,12 +415,12 @@
 def pair_kernel(
     NS, NPD, T, Z, Y,
     u_ref, prec_ref, bound_ref, cap_ref, capacity_ref, bv_ref, tc_ref, dens_ref, slope_ref, om_ref,
-    u_out, prec_out, bound_out, cap_out, w_out,
+    u_out, prec_out, bound_out, few_out,
     praw, hh, pu, pb, pp, hpr, nraw, hnr, bvb, tcb, slr,
     fa, ca, sa, fn, cn, sn, fh, ch, sh, bf, bc, bs, uf, uc, us,
     act, nact, hact, ton, tb, pr, tl, tt, rp, rh,
     xs, xr, hs, ls, zh, zl, dh, dl, rs, rb,
-    loc, ini_s, ini_r, sl_s, sl_r, sm_s, sm_r, re_s, re_r,
+    token, loc, ini_s, ini_r, sl_s, sl_r, sm_s, sm_r, re_s, re_r,
     x_s, x_r, z_s, z_r, d_s, d_r, r_s, r_r, o_s, o_r,
 ):
     me = lax.axis_index("strip")
@@ -478,18 +478,27 @@
         load.start()
     barrier = pltpu.get_barrier_semaphore()
     others = [divmod(k, NPD) for k in range(1, ND)]
+    others.sort(key=lambda o: -abs(o[0] - NS // 2) if o[0] else NS)
 
     def other(ks, kp):
         return {"strip": lax.rem(me + ks, NS), "period": lax.rem(pe + kp, NPD)}
-
-    for ks, kp in others:
-        pl.semaphore_signal(barrier, inc=1, device_id=other(ks, kp), device_id_type=MESH)
 
     mates = [divmod(k, NPD) for k in range(1, NQ)]
 
     def mate(i):
         kh, kp = mates[i]
         return lax.rem(h + kh, 2), lax.rem(pe + kp, NPD)
+
+    has = (a > 0, a < pairs - 1)
+    up = (q > 0, q < NQ - 1)
+    beside = [device_at(a - 1, q), device_at(a + 1, q)]
+    for i in range(NQ - 1):
+        th, tp = mate(i)
+        pl.semaphore_signal(barrier, inc=1, device_id={"strip": 2 * a + th, "period": tp}, device_id_type=MESH)
+    for d in range(2):
+        pl.when(has[d])(
+            lambda d=d: pl.semaphore_signal(barrier, inc=1, device_id=beside[d], device_id_type=MESH)
+        )
 
     def in_ends(what, rows, block, at):
         if what == 1:
@@ -518,24 +527,13 @@
             return remote(tc_ref.at[0, rows], tcb.at[h], sm_s.at[0], sm_r.at[0], dev)
         return remote(bv_ref.at[0, rows], bvb.at[h], sm_s.at[1], sm_r.at[1], dev)
 
-    has = (a > 0, a < pairs - 1)
-
     def slope_copy(what):
-        if what == 0:
-            return remote(slope_ref, slr.at[1 + h], sl_s.at[0], sl_r.at[0], {"strip": 2 * a + 1 - h, "period": pe})
-        away = jnp.where(h == 0, a - 1, a + 1)
-        return remote(
-            slope_ref, slr.at[3 * (1 - h)], sl_s.at[what], sl_r.at[2 - h],
-            {"strip": 2 * away + what - 1, "period": pe},
-        )
-
-    def slope_wait(d):
-        return remote(slope_ref, slr.at[3 * d], sl_s.at[1], sl_r.at[1 + d], {"strip": lax.rem(me + 1, NS), "period": pe})
-
-    has_away = jnp.where(h == 0, a - 1, pairs - 2 - a) >= 0
+        if what == 2:
+            return remote(slope_ref, slr.at[1 + h], sl_s.at[2], sl_r.at[2], {"strip": 2 * a + 1 - h, "period": pe})
+        return remote(slr.at[1 + what], slr.at[3 - 3 * what], sl_s.at[what], sl_r.at[1 - what], beside[what])
 
     def relay_copy(d, what):
-        dev = device_at(a - 1 if d == 0 else a + 1, q)
+        dev = beside[d]
         k, hs_ = (2, 0) if d == 0 else (1, 1)
         ss, rr = re_s.at[d, what], re_r.at[d, what]
         if what == 0:
@@ -562,7 +560,7 @@
         return parts[0]
 
     def x_copy(d, s):
-        dev = device_at(a - 1 if d == 0 else a + 1, q)
+        dev = beside[d]
         return remote(xs.at[s, d], xr.at[s, 1 - d], x_s.at[d], x_r.at[s % 2, 1 - d], dev)
 
     def z_copy(d, s):
@@ -592,8 +590,6 @@
     def out_all(what):
         dst = out_ends(what, 0, mine, pl.ds(0, ROWS * (NQ - 1)))[1]
         return remote(dst, dst, o_s.at[what], o_r.at[what], other(0, 1))
-
-    up = (q > 0, q < NQ - 1)
 
     for d in range(2):
         @pl.when(jnp.logical_not(has[d]))
@@ -656,17 +652,20 @@
         line = jnp.where(lanes1 == pe * T + t, cap_ref[t] * lead, line)
         line = jnp.where(lanes1 == NP + pe * T + t, capacity_ref[t] * lead, line)
 
-    pl.semaphore_wait(barrier, ND - 1)
-    for what in range(2):
+    pl.semaphore_wait(barrier, NQ - 1 + has[0].astype(jnp.int32) + has[1].astype(jnp.int32))
+    start(None, slope_copy(2))
+    for what in range(3):
         for i in range(NQ - 1):
             in_copy(i, what).start()
-    start(None, slope_copy(0))
-    for what in (1, 2):
-        start(has_away, slope_copy(what))
     start(None, partner_copy(0))
     start(None, partner_copy(1))
+    for d in range(2):
+        pl.when(has[1 - d])(lambda d=d: pl.semaphore_wait(token.at[d], 1))
+        pl.when(has[d])(
+            lambda d=d: pl.semaphore_signal(token.at[d], inc=1, device_id=beside[d], device_id_type=MESH)
+        )
     reduce_start(0, line)
-    for what in range(2, 6):
+    for what in range(3, 6):
         for i in range(NQ - 1):
             in_copy(i, what).start()
 
@@ -686,7 +685,9 @@
             ok = ok & (jnp.full((ROWS, Y), inside.astype(jnp.int32)) == 1)
         return ok.astype(jnp.float32)
 
-    wait_recv(None, slope_copy(0))
+    wait_recv(None, slope_copy(2))
+    for d in range(2):
+        start(has[d], slope_copy(d))
     here, below = z_ids + ROWS * q, jnp.full((ROWS, Y), ROWS * (q + 1))
     for hh_ in range(2):
         code = slr[1 + hh_]
@@ -699,7 +700,7 @@
             act[k, hh_] = mask_of(code, k, here, inside)
             hact[k, hh_] = mask_of(code, k, below, inside)
     for d in range(2):
-        wait_recv(has[d], slope_wait(d))
+        wait_recv(has[d], slope_copy(1 - d))
         nact[d] = mask_of(slr[3 * d], 1 + d, here + 1, has[d])
 
     wait_recv(None, partner_copy(0))
@@ -867,7 +868,10 @@
                 part = ton[hh_] * ext
                 mined = part if mined is None else mined + part
             row = jnp.where(rows == t, jnp.sum(mined, axis=0, keepdims=True), row)
-        reduce_start(1 + s, as_lanes(row))
+        if not last:
+            reduce_start(1 + s, as_lanes(row))
+        if final:
+            out_start(0)
         pl.when(up[1])(z_copy(1, s).start)
         for d in range(2):
             pl.when(has[d])(x_copy(d, s).start)
@@ -877,8 +881,8 @@
             pl.when(up[0])(z_copy(0, s).start)
             for d in range(2):
                 pl.when(has[d] & up[0])(d_copy(d, 0, s).start)
-        if final:
-            out_start(0)
+        if last:
+            reduce_start(1 + s, as_lanes(row))
 
         def arc(k, hh_, at, diff, move):
             old = p_src[k, hh_, at]
@@ -916,7 +920,6 @@
             move_d = arc(2, 1, at, c[1] - cz[0], move_d)
         if final:
             out_start(2)
-            out_start(3)
         for d in range(2):
             wait_recv(has[d], x_copy(1 - d, s))
             wait_recv(has[d] & up[0], d_copy(1 - d, 1, s))
@@ -931,6 +934,7 @@
             md = jnp.sum(move_d, axis=0, keepdims=True)
             reduce_start(1 + STEPS + cyc, as_lanes(jnp.where(rows == 0, mp, jnp.where(rows == 1, md, 0.0))))
         if final:
+            out_start(3)
             out_start(4)
         else:
             wait_recv(up[1], z_copy(0, s))
@@ -971,14 +975,13 @@
             cap_move = jnp.sum((caps - cap_first) ** 2, axis=0, keepdims=True)
             if final:
                 for t in range(T):
-                    own = jnp.sum(jnp.where(rows == pe * T + t, caps, 0.0), axis=0, keepdims=True)
-                    cap_out[t] = own[0, 0]
+                    few_out[t] = jnp.sum(jnp.where(rows == pe * T + t, caps, 0.0), axis=0)
             tot = as_rows(reduce_done(1 + STEPS + cyc))
             moved = jnp.sqrt((tot[1:2, :] + cap_move + EPS) / (tot[0:1, :] + EPS))
             w = jnp.sqrt(w * moved)
             if not final:
                 set_rates(w)
-    w_out[0] = w[0, 0]
+    few_out[T] = w[0]
     u_out[0, :, rows_of(q)] = uf[h, mine]
     bound_out[0, :, rows_of(q)] = bf[h, mine]
     for k in range(5):
@@ -1007,6 +1010,22 @@
             copy.wait_send()
         else:
             pl.when(cond)(lambda copy=copy: copy.wait_send())
+
+
+def store_kernel(u_ref, prec_ref, bound_ref, few_ref, u_out, prec_out, bound_out, cap_out, w_out, sem):
+    stores = (
+        pltpu.make_async_copy(prec_ref, prec_out, sem.at[0]),
+        pltpu.make_async_copy(u_ref, u_out, sem.at[1]),
+        pltpu.make_async_copy(bound_ref, bound_out, sem.at[2]),
+    )
+    for store in stores:
+        store.start()
+    T = cap_out.shape[0]
+    for t in range(T):
+        cap_out[t] = few_ref[t, 0]
+    w_out[0] = few_ref[T, 0]
+    for store in stores:
+        store.wait()
 
 
 def pair_call(NS, NPD, u, prec, bound, cap, capacity, bv, tc, dens, slope, om):
@@ -1023,17 +1042,16 @@
     whole = lambda *n: V(*n, NP, ROWS)
     edge = lambda *n: V(*n, NT, ROWS)
     dma = pltpu.SemaphoreType.DMA
-    return pl.pallas_call(
+    ours = pl.pallas_call(
         functools.partial(pair_kernel, NS, NPD, T, Z, Y),
         out_shape=(
             pltpu.VMEM(u.shape, f32),
             pltpu.VMEM(prec.shape, f32),
             pltpu.VMEM(bound.shape, f32),
-            jax.ShapeDtypeStruct(cap.shape, f32),
-            jax.ShapeDtypeStruct((1,), f32),
+            pltpu.VMEM((T + 1, Y), f32),
         ),
         in_specs=[hbm, hbm, hbm, smem, smem, vmem, vmem, smem, vmem, smem],
-        out_specs=(vmem, vmem, vmem, smem, smem),
+        out_specs=(vmem, vmem, vmem, vmem),
         scratch_shapes=[
             V(5, T, Z), V(NQ, 5, T), unit(), unit(), unit(5), V(NQ, 5, T), V(2, NPD, T, ROWS), V(2, NPD, T),
             V(2, ROWS), pltpu.VMEM((2, ROWS, Y), jnp.int32), pltpu.VMEM((4, 1, Y), jnp.int32),
@@ -1043,12 +1061,25 @@
             whole(), edge(),
             whole(STEPS, 2), whole(STEPS, 2), edge(STEPS, 2), edge(STEPS, 2), edge(STEPS, 2), edge(STEPS, 2),
             edge(STEPS, 2), edge(STEPS, 2), V(slots, 1), V(slots, ND, 1),
-            dma((4,)), dma((6,)), dma((6,)), dma((3,)), dma((3,)), dma((2,)), dma((2,)), dma((2, 2)), dma((2, 2)),
+            pltpu.SemaphoreType.REGULAR((2,)), dma((4,)), dma((6,)), dma((6,)), dma((3,)), dma((3,)), dma((2,)), dma((2,)), dma((2, 2)), dma((2, 2)),
             dma((2,)), dma((2, 2)), dma((2,)), dma((2, 2)), dma((2, 2)), dma((2, 2, 2)), dma((1,)), dma((3,)),
             dma((5,)), dma((5,)),
         ],
         compiler_params=pltpu.CompilerParams(collective_id=1, has_side_effects=True),
     )(u, prec, bound, cap, capacity, bv, tc, dens, slope, om)
+    return pl.pallas_call(
+        store_kernel,
+        out_shape=(
+            jax.ShapeDtypeStruct(u.shape, f32),
+            jax.ShapeDtypeStruct(prec.shape, f32),
+            jax.ShapeDtypeStruct(bound.shape, f32),
+            jax.ShapeDtypeStruct(cap.shape, f32),
+            jax.ShapeDtypeStruct((1,), f32),
+        ),
+        in_specs=[vmem] * 4,
+        out_specs=(hbm, hbm, hbm, smem, smem),
+        scratch_shapes=[dma((3,))],
+    )(*[pltpu.with_memory_space_constraint(x, pltpu.VMEM) for x in ours])
 
 
 def solution(mesh):

time: 68 us -> 62.7 us (0.922)
  local copies, waits for them, and re-layouts: 2.66 us -> 0 us
  between operations: 3.05 us -> 1.29 us
  Pallas kernels: 62.1 us -> 61.2 us
    unnamed x6 -> x0, local copies, waits for them, and re-layouts: 2.66 us -> none
    pallas_call x1, Pallas kernels: 62.1 us -> 59.7 us  [pair_call(): pl.pallas_call(functools.partial(pair_kernel, NS, NPD, T, Z, Y), out_shap...]
    pallas_call x0 -> x1, Pallas kernels: none -> 1.47 us  [pair_call(): pl.pallas_call(store_kernel, out_shape=(jax.ShapeDtypeStruct(u.shape, f32...]
where the time goes in v3:
time: 62.7 us; the launch traced here: 62.5 us
  Pallas kernels  61.2 us (98%)
  between operations  1.29 us (2%)
    pallas_call x1, Pallas kernels, pair_call(): pl.pallas_call(functools.partial(pair_kernel, NS, NPD, T, Z, Y), out_shap...  59.7 us
    pallas_call x1, Pallas kernels, pair_call(): pl.pallas_call(store_kernel, out_shape=(jax.ShapeDtypeStruct(u.shape, f32...  1.47 us

profile of v3, /device:TPU:0, one launch (start us, length us, event | category | flops | bytes accessed | tf_op | source)
XLA Modules:
  0.0 62.5 jit_solution(15430156090809660059)
XLA Ops:
  1.3 59.7 %shard_map.137 = (f32[1,4,64,128]{3,2,1,0:T(8,128)S(1)}, f32[5,1,4,64,128]{4,3,2,1,0:T(8,128)S(1)}, f32[1,4,64,128]{3,2,1,0:T(8,128)S(1)}, f32[5,128]{1,0:T(8,128)S(1)}) custom-call(f32[1,4,64,128]{3,2,1,0:T(8,128)} %u_ref.1, f32[5,1,4,64,128]{4,3,2,1,0:T(8,128)} %prec_ref.1, f32[1,4,64,128]{3,2,1,0:T(8,128)} %bound_ref.1, f32[4]{0:T(128)} %cap_ref.1, ...), custom_call_target="tpu_custom_call" | custom-call | tf_op jit(solution)/shard_map/pallas_call | solution.py:1045
  61.0 1.5 %shard_map.138 = (f32[1,4,64,128]{3,2,1,0:T(8,128)}, f32[5,1,4,64,128]{4,3,2,1,0:T(8,128)}, f32[1,4,64,128]{3,2,1,0:T(8,128)}, f32[4]{0:T(128)}, f32[1]{0:T(128)}) custom-call(f32[1,4,64,128]{3,2,1,0:T(8,128)S(1)} %get-tuple-element.9.u_ref, f32[5,1,4,64,128]{4,3,2,1,0:T(8,128)S(1)} %get-tuple-element.10.prec_ref, ...), custom_call_target="tpu_custom_call" | custom-call | tf_op jit(solution)/shard_map/pallas_call | solution.py:1070

commit v4 on v3

--- a/solution.py
+++ b/solution.py
@@ -416,7 +416,7 @@
     NS, NPD, T, Z, Y,
     u_ref, prec_ref, bound_ref, cap_ref, capacity_ref, bv_ref, tc_ref, dens_ref, slope_ref, om_ref,
     u_out, prec_out, bound_out, few_out,
-    praw, hh, pu, pb, pp, hpr, nraw, hnr, bvb, tcb, slr,
+    slope_own, cap_own, capacity_own, dens_own, om_own, cap_line, capb, praw, braw, gh, hh, pu, pb, pg, pp, hpr, nraw, hnr, bvb, tcb, slr,
     fa, ca, sa, fn, cn, sn, fh, ch, sh, bf, bc, bs, uf, uc, us,
     act, nact, hact, ton, tb, pr, tl, tt, rp, rh,
     xs, xr, hs, ls, zh, zl, dh, dl, rs, rb,
@@ -473,6 +473,14 @@
         pltpu.make_async_copy(prec_ref.at[:, 0, :, rows_of(q)], pp.at[:, unit], loc.at[1]),
         pltpu.make_async_copy(bound_ref.at[0, :, rows_of(q)], pb.at[unit], loc.at[2]),
         pltpu.make_async_copy(u_ref.at[0, :, rows_of(q)], pu.at[unit], loc.at[3]),
+        pltpu.make_async_copy(bound_ref.at[0], braw, loc.at[4]),
+        pltpu.make_async_copy(slope_ref, slope_own, loc.at[5]),
+        pltpu.make_async_copy(cap_ref, cap_own, loc.at[6]),
+        pltpu.make_async_copy(capacity_ref, capacity_own, loc.at[7]),
+        pltpu.make_async_copy(dens_ref, dens_own, loc.at[8]),
+        pltpu.make_async_copy(om_ref, om_own, loc.at[9]),
+        pltpu.make_async_copy(bv_ref.at[0, rows_of(q)], bvb.at[h], loc.at[10]),
+        pltpu.make_async_copy(tc_ref.at[0, rows_of(q)], tcb.at[h], loc.at[11]),
     )
     for load in loads:
         load.start()
@@ -503,11 +511,15 @@
     def in_ends(what, rows, block, at):
         if what == 1:
             return hh.at[block], hpr.at[at]
+        if what == 2:
+            return gh.at[:, rows], pg.at[at]
+        if what == 7:
+            return cap_line, capb.at[at]
+        if what == 3:
+            return u_ref.at[0, :, rows], pu.at[at]
         if what == 4:
             return bound_ref.at[0, :, rows], pb.at[at]
-        if what == 5:
-            return u_ref.at[0, :, rows], pu.at[at]
-        arcs = (pl.ds(1, 2), None, 0, pl.ds(3, 2))[what]
+        arcs = {0: pl.ds(1, 2), 5: 0, 6: pl.ds(3, 2)}[what]
         return prec_ref.at[arcs, 0, :, rows], pp.at[arcs, at]
 
     def in_copy(i, what):
@@ -541,7 +553,7 @@
         return remote(hpr.at[pl.ds(hs_ * NPD, NPD), k], hnr.at[1 - d], ss, rr, dev)
 
     def reduce_sem(slot):
-        return r_r.at[slot % 2 if slot <= STEPS else 2]
+        return r_r.at[slot % 2 if slot < STEPS else 2]
 
     def reduce_start(slot, value):
         rs[slot] = value
@@ -591,6 +603,86 @@
         dst = out_ends(what, 0, mine, pl.ds(0, ROWS * (NQ - 1)))[1]
         return remote(dst, dst, o_s.at[what], o_r.at[what], other(0, 1))
 
+    lanes1 = lax.broadcasted_iota(jnp.int32, (1, Y), 1)
+    rows = lax.broadcasted_iota(jnp.int32, (NP, Y), 0)
+    lanes = lax.broadcasted_iota(jnp.int32, (NP, Y), 1)
+
+    def tons_of(cls):
+        tons = jnp.zeros(cls.shape, jnp.float32)
+        for c in range(dens_own.shape[0]):
+            tons = jnp.where(cls == c, (1.0 + c) * dens_own[c], tons)
+        return tons
+
+    def as_lanes(value):
+        sums = jnp.sum(value, axis=1, keepdims=True)
+        return jnp.sum(jnp.where(lanes == rows, sums, 0.0), axis=0, keepdims=True)
+
+    def as_rows(line, at=0):
+        return jnp.broadcast_to(jnp.sum(jnp.where(lanes == rows + at, line, 0.0), axis=1, keepdims=True), (NP, Y))
+
+    def roll(v, by, axis):
+        return pltpu.roll(v, by % v.shape[axis], axis)
+
+    def up_y(v):
+        return roll(v, 1, v.ndim - 1)
+
+    def dn_y(v):
+        return roll(v, -1, v.ndim - 1)
+
+    def mask_of(code, k, depth, inside):
+        ok = (depth >= 1) & (depth < Z)
+        y_ids = lax.broadcasted_iota(jnp.int32, depth.shape, 1)
+        if k > 0:
+            ok = ok & (jnp.broadcast_to((code >> (k - 1)) & 1, depth.shape) == 1)
+        if k == 3:
+            ok = ok & (y_ids < Y - 1)
+        if k == 4:
+            ok = ok & (y_ids >= 1)
+        if inside is not None:
+            ok = ok & (jnp.full(depth.shape, inside.astype(jnp.int32)) == 1)
+        return ok.astype(jnp.float32)
+
+    def send_all(*kinds):
+        for what in kinds:
+            for i in range(NQ - 1):
+                in_copy(i, what).start()
+
+    pl.semaphore_wait(barrier, NQ - 1 + has[0].astype(jnp.int32) + has[1].astype(jnp.int32))
+    send_all(0)
+    start(None, slope_copy(2))
+    start(None, partner_copy(0))
+    start(None, partner_copy(1))
+    send_all(3)
+    for load in loads[6:10]:
+        load.wait()
+    line = jnp.zeros((1, Y), jnp.float32)
+    for t in range(T):
+        line = jnp.where(lanes1 == pe * T + t, cap_own[t], line)
+        line = jnp.where(lanes1 == NP + pe * T + t, capacity_own[t], line)
+    cap_line[...] = line
+    capb[unit] = line
+    loads[0].wait()
+    for b in range(NQ):
+        if b + 1 < NQ:
+            for k in range(5):
+                for t in range(T):
+                    hh[b, k, pl.ds(t, 1)] = praw[k, t, pl.ds(ROWS * (b + 1), 1)]
+        else:
+            hh[b] = jnp.zeros((5, T, Y), jnp.float32)
+    hpr[unit] = hh[q]
+    send_all(1, 7)
+    z_ids = lax.broadcasted_iota(jnp.int32, (ROWS, Y), 0)
+    low = z_ids == ROWS - 1
+    depth = lax.broadcasted_iota(jnp.int32, (Z, Y), 0)
+    loads[5].wait()
+    home = {k: mask_of(slope_own[...], k, depth, None) for k in (0, 3, 4)}
+    loads[4].wait()
+    for t in range(T):
+        p0, p3, p4 = (praw[k, t] * home[k] for k in (0, 3, 4))
+        gh[t] = ((p0 + p3) + (p4 + braw[t])) - roll(p0 + (up_y(p3) + dn_y(p4)), -1, 0)
+    pg[unit] = gh[:, rows_of(q)]
+    send_all(2, 4, 5)
+    slr[1 + h] = slope_own[...]
     for d in range(2):
         @pl.when(jnp.logical_not(has[d]))
         def _():
@@ -613,77 +705,6 @@
         def _():
             for s in range(STEPS):
                 buf[s] = jnp.zeros((2, NT, ROWS, Y), jnp.float32)
-
-    lanes1 = lax.broadcasted_iota(jnp.int32, (1, Y), 1)
-    rows = lax.broadcasted_iota(jnp.int32, (NP, Y), 0)
-    lanes = lax.broadcasted_iota(jnp.int32, (NP, Y), 1)
-
-    def tons_of(cls):
-        tons = jnp.zeros(cls.shape, jnp.float32)
-        for c in range(dens_ref.shape[0]):
-            tons = jnp.where(cls == c, (1.0 + c) * dens_ref[c], tons)
-        return tons
-
-    def as_lanes(value):
-        sums = jnp.sum(value, axis=1, keepdims=True)
-        return jnp.sum(jnp.where(lanes == rows, sums, 0.0), axis=0, keepdims=True)
-
-    def as_rows(line, at=0):
-        return jnp.broadcast_to(jnp.sum(jnp.where(lanes == rows + at, line, 0.0), axis=1, keepdims=True), (NP, Y))
-
-    slr[1 + h] = slope_ref[...]
-    loads[0].wait()
-    for b in range(NQ):
-        if b + 1 < NQ:
-            for k in range(5):
-                for t in range(T):
-                    hh[b, k, pl.ds(t, 1)] = praw[k, t, pl.ds(ROWS * (b + 1), 1)]
-        else:
-            hh[b] = jnp.zeros((5, T, Y), jnp.float32)
-    hpr[unit] = hh[q]
-    bvb[h] = bv_ref[0, rows_of(q)]
-    tcb[h] = tc_ref[0, rows_of(q)]
-    deep = Z // NPD
-    strip_part = tons_of(tc_ref[0, pl.ds(pl.multiple_of(pe * deep, ROWS), deep)])
-    strip_part = jnp.sum(jnp.sum(strip_part, axis=0, keepdims=True), axis=1, keepdims=True)
-    line = jnp.where(lanes1 == 2 * NP, strip_part, 0.0)
-    lead = jnp.where(me == 0, 1.0, 0.0)
-    for t in range(T):
-        line = jnp.where(lanes1 == pe * T + t, cap_ref[t] * lead, line)
-        line = jnp.where(lanes1 == NP + pe * T + t, capacity_ref[t] * lead, line)
-
-    pl.semaphore_wait(barrier, NQ - 1 + has[0].astype(jnp.int32) + has[1].astype(jnp.int32))
-    start(None, slope_copy(2))
-    for what in range(3):
-        for i in range(NQ - 1):
-            in_copy(i, what).start()
-    start(None, partner_copy(0))
-    start(None, partner_copy(1))
-    for d in range(2):
-        pl.when(has[1 - d])(lambda d=d: pl.semaphore_wait(token.at[d], 1))
-        pl.when(has[d])(
-            lambda d=d: pl.semaphore_signal(token.at[d], inc=1, device_id=beside[d], device_id_type=MESH)
-        )
-    reduce_start(0, line)
-    for what in range(3, 6):
-        for i in range(NQ - 1):
-            in_copy(i, what).start()
-
-    z_ids = lax.broadcasted_iota(jnp.int32, (ROWS, Y), 0)
-    y_ids = lax.broadcasted_iota(jnp.int32, (ROWS, Y), 1)
-    low = z_ids == ROWS - 1
-
-    def mask_of(code, k, depth, inside):
-        ok = (depth >= 1) & (depth < Z)
-        if k > 0:
-            ok = ok & (jnp.broadcast_to((code >> (k - 1)) & 1, (ROWS, Y)) == 1)
-        if k == 3:
-            ok = ok & (y_ids < Y - 1)
-        if k == 4:
-            ok = ok & (y_ids >= 1)
-        if inside is not None:
-            ok = ok & (jnp.full((ROWS, Y), inside.astype(jnp.int32)) == 1)
-        return ok.astype(jnp.float32)
 
     wait_recv(None, slope_copy(2))
     for d in range(2):
@@ -705,6 +726,8 @@
 
     wait_recv(None, partner_copy(0))
     wait_recv(None, partner_copy(1))
+    loads[10].wait()
+    loads[11].wait()
     for hh_ in range(2):
         tons = tons_of(tcb[hh_])
         ton[hh_] = tons
@@ -717,7 +740,7 @@
         lax.broadcasted_iota(jnp.int32, (NT, ROWS, Y), 0) * ROWS + lax.broadcasted_iota(jnp.int32, (NT, ROWS, Y), 1)
     ).astype(jnp.float32)
 
-    w = jnp.full((1, Y), om_ref[0])
+    w = jnp.full((1, Y), om_own[0])
 
     def set_rates(w):
         rp[...] = w[None] / (2.0 * (t_plane + 1.0))
@@ -725,6 +748,11 @@
 
     set_rates(w)
 
+    for d in range(2):
+        pl.when(has[1 - d])(lambda d=d: pl.semaphore_wait(token.at[d], 1))
+        pl.when(has[d])(
+            lambda d=d: pl.semaphore_signal(token.at[d], inc=1, device_id=beside[d], device_id_type=MESH)
+        )
     loads[1].wait()
     in_all(0).wait_recv()
     for d in range(2):
@@ -734,15 +762,6 @@
         start(has[d], relay_copy(d, 1))
 
     chunks = [(lo, min(CHUNK, NP - lo)) for lo in range(0, NP, CHUNK)]
-
-    def roll(v, by, axis):
-        return pltpu.roll(v, by % v.shape[axis], axis)
-
-    def up_y(v):
-        return roll(v, 1, v.ndim - 1)
-
-    def dn_y(v):
-        return roll(v, -1, v.ndim - 1)
 
     def lines(ref, lo, size, *at):
         picked = [ref[(*at, t // ROWS, pl.ds(t % ROWS, 1))] for t in range(lo, lo + size)]
@@ -762,25 +781,20 @@
             for hh_ in range(2):
                 fa[k, hh_] = landed(pp, hh_, k) * act[k, hh_][None]
 
+    def mask_halo(ks):
+        for k, hh_ in ks:
+            for at in range(NP):
+                line = hpr[hh_ * NPD + at // T, k, pl.ds(at % T, 1)]
+                fh[k, hh_, at // ROWS, pl.ds(at % ROWS, 1)] = line * hact[k, hh_, 0:1]
+
     mask_arcs((1, 2))
-    in_all(2).wait_recv()
-    mask_arcs((0,))
-    in_all(3).wait_recv()
-    mask_arcs((3, 4))
-    for k in range(5):
-        for hh_ in range(2):
-            for p in range(NPD):
-                for t in range(T):
-                    at = p * T + t
-                    fh[k, hh_, at // ROWS, pl.ds(at % ROWS, 1)] = hpr[hh_ * NPD + p, k, pl.ds(t, 1)] * hact[k, hh_, 0:1]
+    mask_halo(((1, 0), (2, 1)))
     for d in range(2):
         wait_recv(has[d], relay_copy(1 - d, 0))
         wait_recv(has[d], relay_copy(1 - d, 1))
         for t in range(NP):
             edge = jnp.broadcast_to(hnr[d, t // T, pl.ds(t % T, 1)], (ROWS, Y))
             fn[d, t] = jnp.where(low, edge, roll(nraw[d, t // T, t % T], -1, 0)) * nact[d]
-    loads[2].wait()
-    in_all(4).wait_recv()
 
     def settle(first, cur, acc, at, j, new, old):
         if j == 0:
@@ -795,37 +809,56 @@
         first[at] = mean
         return jnp.sum(diff * diff, axis=0)
 
+    def rows_under(edge, lo, size):
+        return jnp.stack([
+            jnp.broadcast_to(edge[t // ROWS, t % ROWS : t % ROWS + 1], (ROWS, Y)) for t in range(lo, lo + size)
+        ])
+
     def gradient(arcs, near, halo, bounds):
         for hh_ in range(2):
-            k_in = 2 if hh_ == 0 else 1
+            k_in = 2 - hh_
             edge = (halo[0, hh_] + halo[k_in, 1 - hh_]) + (up_y(halo[3, hh_]) + dn_y(halo[4, hh_]))
-            hs_tmp = edge
             tail = None
             for lo, size in reversed(chunks):
                 at = pl.ds(lo, size)
                 p0, p3, p4 = arcs[0, hh_, at], arcs[3, hh_, at], arcs[4, hh_, at]
                 back = (p0 + arcs[k_in, 1 - hh_, at]) + (up_y(p3) + dn_y(p4))
-                rows_below = jnp.stack([
-                    jnp.broadcast_to(hs_tmp[t // ROWS, t % ROWS : t % ROWS + 1], (ROWS, Y)) for t in range(lo, lo + size)
-                ])
                 g = ((p0 + p3) + (p4 + bounds[hh_, at])) + (arcs[1, hh_, at] + arcs[2, hh_, at])
-                g = g - (from_below(back, rows_below) + near[hh_, at])
+                g = g - (from_below(back, rows_under(edge, lo, size)) + near[hh_, at])
                 for t in range(lo + size - 1, lo - 1, -1):
                     tail = g[t - lo] if tail is None else tail + g[t - lo]
                     tl[hh_, t] = tail
 
+    in_all(2).wait_recv()
     for hh_ in range(2):
-        bf[hh_] = landed(pb, hh_)
-    gradient(fa, fn, fh, bf)
+        k_in = 2 - hh_
+        edge = fh[k_in, 1 - hh_]
+        tail = None
+        for lo, size in reversed(chunks):
+            at = pl.ds(lo, size)
+            g = landed(pg, hh_)[lo : lo + size] + (fa[1, hh_, at] + fa[2, hh_, at])
+            g = g - (from_below(fa[k_in, 1 - hh_, at], rows_under(edge, lo, size)) + fn[hh_, at])
+            for t in range(lo + size - 1, lo - 1, -1):
+                tail = g[t - lo] if tail is None else tail + g[t - lo]
+                tl[hh_, t] = tail
     loads[3].wait()
-    in_all(5).wait_recv()
+    in_all(3).wait_recv()
     for hh_ in range(2):
         uf[hh_] = landed(pu, hh_)
-    got = reduce_done(0)
+    in_all(7).wait_recv()
+    got = capb[0]
+    for p in range(1, NPD):
+        got = got + capb[p]
     caps = as_rows(got)
     climit = as_rows(got, NP) * blocks_all
-    inv_tons = 1.0 / jnp.sum(jnp.where(lanes1 == 2 * NP, got, 0.0), axis=1, keepdims=True)
-    cap_first = cap_sum = None
+    cap_first = cap_sum = inv_tons = None
+
+    def totals(row, s):
+        line = as_lanes(row)
+        if s > 0:
+            return line
+        tons = jnp.sum(jnp.sum(ton[0] + ton[1], axis=0, keepdims=True), axis=1, keepdims=True)
+        return jnp.where(lanes1 == NP, tons, line)
 
     for s in range(STEPS):
         j = s % INNER
@@ -869,7 +902,7 @@
                 mined = part if mined is None else mined + part
             row = jnp.where(rows == t, jnp.sum(mined, axis=0, keepdims=True), row)
         if not last:
-            reduce_start(1 + s, as_lanes(row))
+            reduce_start(s, totals(row, s))
         if final:
             out_start(0)
         pl.when(up[1])(z_copy(1, s).start)
@@ -881,8 +914,14 @@
             pl.when(up[0])(z_copy(0, s).start)
             for d in range(2):
                 pl.when(has[d] & up[0])(d_copy(d, 0, s).start)
+        if s == 0:
+            send_all(6)
+            loads[2].wait()
+            in_all(4).wait_recv()
+            for hh_ in range(2):
+                bf[hh_] = landed(pb, hh_)
         if last:
-            reduce_start(1 + s, as_lanes(row))
+            reduce_start(s, totals(row, s))
 
         def arc(k, hh_, at, diff, move):
             old = p_src[k, hh_, at]
@@ -908,14 +947,24 @@
         if final:
             out_start(1)
         wait_recv(up[0], z_copy(1, s))
+
+        def own_arcs(move):
+            for lo, size in chunks:
+                at = pl.ds(lo, size)
+                for hh_ in range(2):
+                    c = xs[s, hh_, at]
+                    cz = from_above(c, lines(zh, lo, size, s, hh_))
+                    move = arc(0, hh_, at, c - cz, move)
+                    move = arc(3, hh_, at, c - dn_y(cz), move)
+                    move = arc(4, hh_, at, c - up_y(cz), move)
+            return move
+
+        if s > 0:
+            move_d = own_arcs(move_d)
         for lo, size in chunks:
             at = pl.ds(lo, size)
             c = [xs[s, hh_, at] for hh_ in range(2)]
             cz = [from_above(c[hh_], lines(zh, lo, size, s, hh_)) for hh_ in range(2)]
-            for hh_ in range(2):
-                move_d = arc(0, hh_, at, c[hh_] - cz[hh_], move_d)
-                move_d = arc(3, hh_, at, c[hh_] - dn_y(cz[hh_]), move_d)
-                move_d = arc(4, hh_, at, c[hh_] - up_y(cz[hh_]), move_d)
             move_d = arc(1, 0, at, c[0] - cz[1], move_d)
             move_d = arc(2, 1, at, c[1] - cz[0], move_d)
         if final:
@@ -932,7 +981,7 @@
             cyc = s // INNER
             mp = jnp.sum(move_p, axis=0, keepdims=True)
             md = jnp.sum(move_d, axis=0, keepdims=True)
-            reduce_start(1 + STEPS + cyc, as_lanes(jnp.where(rows == 0, mp, jnp.where(rows == 1, md, 0.0))))
+            reduce_start(STEPS + cyc, as_lanes(jnp.where(rows == 0, mp, jnp.where(rows == 1, md, 0.0))))
         if final:
             out_start(3)
             out_start(4)
@@ -947,6 +996,12 @@
                     diff = from_below(xr[s, d, at], lines(dl, lo, size, s, d)) - xs[s, d, at]
                     new = jnp.maximum(old + rp[at] * diff, 0.0) * nact[d][None]
                     settle(fn, cn, sn, (d, at), j, new, old)
+            if s == 0:
+                in_all(5).wait_recv()
+                in_all(6).wait_recv()
+                mask_arcs((0, 3, 4))
+                mask_halo([(k, hh_) for k in (0, 3, 4) for hh_ in range(2)])
+                own_arcs(move_d)
             for hh_ in range(2):
                 c, cz = zl[s, hh_], hs[s, hh_]
                 for k in (0, 3, 4, 1 + hh_):
@@ -962,7 +1017,10 @@
                     for t in range(NP):
                         tau = tb[hh_, t] * inv_w
                         tl[hh_, t] = uc[hh_, t] - tau * (tl[hh_, t] - pr[hh_, t])
-        row_total = as_rows(reduce_done(1 + s))
+        got = reduce_done(s)
+        if s == 0:
+            inv_tons = 1.0 / jnp.sum(jnp.where(lanes1 == NP, got, 0.0), axis=1, keepdims=True)
+        row_total = as_rows(got)
         new_caps = jnp.maximum(caps + w * ((row_total - climit) * inv_tons), 0.0)
         if j == 0:
             cap_first = caps
@@ -976,7 +1034,7 @@
             if final:
                 for t in range(T):
                     few_out[t] = jnp.sum(jnp.where(rows == pe * T + t, caps, 0.0), axis=0)
-            tot = as_rows(reduce_done(1 + STEPS + cyc))
+            tot = as_rows(reduce_done(STEPS + cyc))
             moved = jnp.sqrt((tot[1:2, :] + cap_move + EPS) / (tot[0:1, :] + EPS))
             w = jnp.sqrt(w * moved)
             if not final:
@@ -990,7 +1048,7 @@
         out_all(what).wait_recv()
     for what in range(5):
         out_all(what).wait_send()
-    for what in range(6):
+    for what in range(8):
         in_all(what).wait_send()
     rest = rb.at[:, pl.ds(0, ND - 1)]
     remote(rest, rest, r_s.at[0], r_r.at[0], other(0, 1)).wait_send()
@@ -1036,7 +1094,7 @@
     vmem = pl.BlockSpec(memory_space=pltpu.VMEM)
     hbm = pl.BlockSpec(memory_space=pl.ANY)
     smem = pl.BlockSpec(memory_space=pltpu.SMEM)
-    slots = 1 + STEPS + OUTER
+    slots = STEPS + OUTER
     V = lambda *shape: pltpu.VMEM((*shape, Y), f32)
     unit = lambda *n: V(*n, NQ, T, ROWS)
     whole = lambda *n: V(*n, NP, ROWS)
@@ -1050,10 +1108,12 @@
             pltpu.VMEM(bound.shape, f32),
             pltpu.VMEM((T + 1, Y), f32),
         ),
-        in_specs=[hbm, hbm, hbm, smem, smem, vmem, vmem, smem, vmem, smem],
+        in_specs=[hbm] * 10,
         out_specs=(vmem, vmem, vmem, vmem),
         scratch_shapes=[
-            V(5, T, Z), V(NQ, 5, T), unit(), unit(), unit(5), V(NQ, 5, T), V(2, NPD, T, ROWS), V(2, NPD, T),
+            pltpu.VMEM((1, Y), jnp.int32), pltpu.SMEM(cap.shape, f32), pltpu.SMEM(cap.shape, f32),
+            pltpu.SMEM(dens.shape, f32), pltpu.SMEM(om.shape, f32), V(1), V(NQ, 1),
+            V(5, T, Z), V(T, Z), V(T, Z), V(NQ, 5, T), unit(), unit(), unit(), unit(5), V(NQ, 5, T), V(2, NPD, T, ROWS), V(2, NPD, T),
             V(2, ROWS), pltpu.VMEM((2, ROWS, Y), jnp.int32), pltpu.VMEM((4, 1, Y), jnp.int32),
             whole(5, 2), whole(5, 2), whole(5, 2), whole(2), whole(2), whole(2),
             edge(5, 2), edge(5, 2), edge(5, 2), whole(2), whole(2), whole(2), whole(2), whole(2), whole(2),
@@ -1061,7 +1121,7 @@
             whole(), edge(),
             whole(STEPS, 2), whole(STEPS, 2), edge(STEPS, 2), edge(STEPS, 2), edge(STEPS, 2), edge(STEPS, 2),
             edge(STEPS, 2), edge(STEPS, 2), V(slots, 1), V(slots, ND, 1),
-            pltpu.SemaphoreType.REGULAR((2,)), dma((4,)), dma((6,)), dma((6,)), dma((3,)), dma((3,)), dma((2,)), dma((2,)), dma((2, 2)), dma((2, 2)),
+            pltpu.SemaphoreType.REGULAR((2,)), dma((12,)), dma((8,)), dma((8,)), dma((3,)), dma((3,)), dma((2,)), dma((2,)), dma((2, 2)), dma((2, 2)),
             dma((2,)), dma((2, 2)), dma((2,)), dma((2, 2)), dma((2, 2)), dma((2, 2, 2)), dma((1,)), dma((3,)),
             dma((5,)), dma((5,)),
         ],

time: 62.7 us -> 66.4 us (1.059)
  Pallas kernels: 61.2 us -> 64.9 us
    pallas_call x1, Pallas kernels: 59.7 us -> 63.4 us  [pair_call(): pl.pallas_call(functools.partial(pair_kernel, NS, NPD, T, Z, Y), out_shap...]
where the time goes in v4:
time: 66.4 us; the launch traced here: 66.2 us
  Pallas kernels  64.9 us (98%)
  between operations  1.29 us (2%)
    pallas_call x1, Pallas kernels, pair_call(): pl.pallas_call(functools.partial(pair_kernel, NS, NPD, T, Z, Y), out_shap...  63.4 us
    pallas_call x1, Pallas kernels, pair_call(): pl.pallas_call(store_kernel, out_shape=(jax.ShapeDtypeStruct(u.shape, f32...  1.47 us

profile of v4, /device:TPU:0, one launch (start us, length us, event | category | flops | bytes accessed | tf_op | source)
XLA Modules:
  0.0 66.2 jit_solution(5949476944204048339)
XLA Ops:
  1.3 63.4 %shard_map.137 = (f32[1,4,64,128]{3,2,1,0:T(8,128)S(1)}, f32[5,1,4,64,128]{4,3,2,1,0:T(8,128)S(1)}, f32[1,4,64,128]{3,2,1,0:T(8,128)S(1)}, f32[5,128]{1,0:T(8,128)S(1)}) custom-call(f32[1,4,64,128]{3,2,1,0:T(8,128)} %u_ref.1, f32[5,1,4,64,128]{4,3,2,1,0:T(8,128)} %prec_ref.1, f32[1,4,64,128]{3,2,1,0:T(8,128)} %bound_ref.1, f32[4]{0:T(128)} %cap_ref.1, ...), custom_call_target="tpu_custom_call" | custom-call | tf_op jit(solution)/shard_map/pallas_call | solution.py:1103
  64.7 1.5 %shard_map.138 = (f32[1,4,64,128]{3,2,1,0:T(8,128)}, f32[5,1,4,64,128]{4,3,2,1,0:T(8,128)}, f32[1,4,64,128]{3,2,1,0:T(8,128)}, f32[4]{0:T(128)}, f32[1]{0:T(128)}) custom-call(f32[1,4,64,128]{3,2,1,0:T(8,128)S(1)} %get-tuple-element.9.u_ref, f32[5,1,4,64,128]{4,3,2,1,0:T(8,128)S(1)} %get-tuple-element.10.prec_ref, ...), custom_call_target="tpu_custom_call" | custom-call | tf_op jit(solution)/shard_map/pallas_call | solution.py:1130

commit v5 on v4

--- a/solution.py
+++ b/solution.py
@@ -503,10 +503,9 @@
     for i in range(NQ - 1):
         th, tp = mate(i)
         pl.semaphore_signal(barrier, inc=1, device_id={"strip": 2 * a + th, "period": tp}, device_id_type=MESH)
-    for d in range(2):
-        pl.when(has[d])(
-            lambda d=d: pl.semaphore_signal(barrier, inc=1, device_id=beside[d], device_id_type=MESH)
-        )
+    column = [device_at(lax.rem(a + k, pairs), q) for k in range(1, pairs)]
+    for there in column:
+        pl.semaphore_signal(barrier, inc=1, device_id=there, device_id_type=MESH)
 
     def in_ends(what, rows, block, at):
         if what == 1:
@@ -647,8 +646,10 @@
             for i in range(NQ - 1):
                 in_copy(i, what).start()
 
-    pl.semaphore_wait(barrier, NQ - 1 + has[0].astype(jnp.int32) + has[1].astype(jnp.int32))
+    pl.semaphore_wait(barrier, NQ - 1 + pairs - 1)
     send_all(0)
+    for there in column:
+        pl.semaphore_signal(token.at[0], inc=1, device_id=there, device_id_type=MESH)
     start(None, slope_copy(2))
     start(None, partner_copy(0))
     start(None, partner_copy(1))
@@ -748,11 +749,6 @@
 
     set_rates(w)
 
-    for d in range(2):
-        pl.when(has[1 - d])(lambda d=d: pl.semaphore_wait(token.at[d], 1))
-        pl.when(has[d])(
-            lambda d=d: pl.semaphore_signal(token.at[d], inc=1, device_id=beside[d], device_id_type=MESH)
-        )
     loads[1].wait()
     in_all(0).wait_recv()
     for d in range(2):
@@ -846,6 +842,8 @@
     for hh_ in range(2):
         uf[hh_] = landed(pu, hh_)
     in_all(7).wait_recv()
+    if pairs > 1:
+        pl.semaphore_wait(token.at[0], pairs - 1)
     got = capb[0]
     for p in range(1, NPD):
         got = got + capb[p]
@@ -1121,7 +1119,7 @@
             whole(), edge(),
             whole(STEPS, 2), whole(STEPS, 2), edge(STEPS, 2), edge(STEPS, 2), edge(STEPS, 2), edge(STEPS, 2),
             edge(STEPS, 2), edge(STEPS, 2), V(slots, 1), V(slots, ND, 1),
-            pltpu.SemaphoreType.REGULAR((2,)), dma((12,)), dma((8,)), dma((8,)), dma((3,)), dma((3,)), dma((2,)), dma((2,)), dma((2, 2)), dma((2, 2)),
+            pltpu.SemaphoreType.REGULAR((1,)), dma((12,)), dma((8,)), dma((8,)), dma((3,)), dma((3,)), dma((2,)), dma((2,)), dma((2, 2)), dma((2, 2)),
             dma((2,)), dma((2, 2)), dma((2,)), dma((2, 2)), dma((2, 2)), dma((2, 2, 2)), dma((1,)), dma((3,)),
             dma((5,)), dma((5,)),
         ],

time: 66.4 us -> 61.3 us (0.923)
  Pallas kernels: 64.9 us -> 59.9 us
    pallas_call x1, Pallas kernels: 63.4 us -> 58.4 us  [pair_call(): pl.pallas_call(functools.partial(pair_kernel, NS, NPD, T, Z, Y), out_shap...]
where the time goes in v5:
time: 61.3 us; the launch traced here: 61.2 us
  Pallas kernels  59.9 us (98%)
  between operations  1.29 us (2%)
    pallas_call x1, Pallas kernels, pair_call(): pl.pallas_call(functools.partial(pair_kernel, NS, NPD, T, Z, Y), out_shap...  58.4 us
    pallas_call x1, Pallas kernels, pair_call(): pl.pallas_call(store_kernel, out_shape=(jax.ShapeDtypeStruct(u.shape, f32...  1.47 us

profile of v5, /device:TPU:0, one launch (start us, length us, event | category | flops | bytes accessed | tf_op | source)
XLA Modules:
  0.0 61.2 jit_solution(11357084472389228024)
XLA Ops:
  1.3 58.4 %shard_map.137 = (f32[1,4,64,128]{3,2,1,0:T(8,128)S(1)}, f32[5,1,4,64,128]{4,3,2,1,0:T(8,128)S(1)}, f32[1,4,64,128]{3,2,1,0:T(8,128)S(1)}, f32[5,128]{1,0:T(8,128)S(1)}) custom-call(f32[1,4,64,128]{3,2,1,0:T(8,128)} %u_ref.1, f32[5,1,4,64,128]{4,3,2,1,0:T(8,128)} %prec_ref.1, f32[1,4,64,128]{3,2,1,0:T(8,128)} %bound_ref.1, f32[4]{0:T(128)} %cap_ref.1, ...), custom_call_target="tpu_custom_call" | custom-call | tf_op jit(solution)/shard_map/pallas_call | solution.py:1101
  59.7 1.5 %shard_map.138 = (f32[1,4,64,128]{3,2,1,0:T(8,128)}, f32[5,1,4,64,128]{4,3,2,1,0:T(8,128)}, f32[1,4,64,128]{3,2,1,0:T(8,128)}, f32[4]{0:T(128)}, f32[1]{0:T(128)}) custom-call(f32[1,4,64,128]{3,2,1,0:T(8,128)S(1)} %get-tuple-element.9.u_ref, f32[5,1,4,64,128]{4,3,2,1,0:T(8,128)S(1)} %get-tuple-element.10.prec_ref, ...), custom_call_target="tpu_custom_call" | custom-call | tf_op jit(solution)/shard_map/pallas_call | solution.py:1128

commit v6 on v5

--- a/solution.py
+++ b/solution.py
@@ -416,12 +416,12 @@
     NS, NPD, T, Z, Y,
     u_ref, prec_ref, bound_ref, cap_ref, capacity_ref, bv_ref, tc_ref, dens_ref, slope_ref, om_ref,
     u_out, prec_out, bound_out, few_out,
-    slope_own, cap_own, capacity_own, dens_own, om_own, cap_line, capb, praw, braw, gh, hh, pu, pb, pg, pp, hpr, nraw, hnr, bvb, tcb, slr,
+    slope_own, cap_own, capacity_own, dens_own, om_own, cap_line, capb, hm, hf, hcur, hacc, hc, praw, braw, gh, hh, pu, pb, pg, pp, hpr, nraw, hnr, bvb, tcb, slr,
     fa, ca, sa, fn, cn, sn, fh, ch, sh, bf, bc, bs, uf, uc, us,
     act, nact, hact, ton, tb, pr, tl, tt, rp, rh,
     xs, xr, hs, ls, zh, zl, dh, dl, rs, rb,
     token, loc, ini_s, ini_r, sl_s, sl_r, sm_s, sm_r, re_s, re_r,
-    x_s, x_r, z_s, z_r, d_s, d_r, r_s, r_r, o_s, o_r,
+    x_s, x_r, z_s, z_r, d_s, d_r, r_s, r_r, o_s, o_r, f_s, f_r, c_s, c_r,
 ):
     me = lax.axis_index("strip")
     pe = lax.axis_index("period")
@@ -587,16 +587,60 @@
     def out_ends(what, th, part, rows):
         if what == 0:
             return uf.at[th, part], u_out.at[0, :, rows]
-        if what == 1:
-            return bf.at[th, part], bound_out.at[0, :, rows]
-        arcs = (0, pl.ds(3, 2), pl.ds(1, 2))[what - 2]
-        return fa.at[arcs, th, part], prec_out.at[arcs, 0, :, rows]
-
-    def out_start(what):
+        return fa.at[pl.ds(1, 2), th, part], prec_out.at[pl.ds(1, 2), 0, :, rows]
+
+    def to_mates(src_of, dst, ss, rr):
         for i in range(NQ - 1):
             th, tp = mate(i)
-            src, dst = out_ends(what, th, pl.ds(tp * T, T), rows_of(q))
-            remote(src, dst, o_s.at[what], o_r.at[what], {"strip": 2 * a + th, "period": tp}).start()
+            remote(src_of(th, pl.ds(tp * T, T)), dst, ss, rr, {"strip": 2 * a + th, "period": tp}).start()
+
+    def out_start(what):
+        dst = out_ends(what, 0, mine, rows_of(q))[1]
+        to_mates(lambda th, part: out_ends(what, th, part, rows_of(q))[0], dst, o_s.at[what], o_r.at[what])
+
+    def home_start():
+        here = rows_of(q)
+        for src, at in ((fa.at[0], 0), (fa.at[pl.ds(3, 2)], pl.ds(1, 2)), (bf, 3)):
+            pick = lambda th, part: src.at[:, th, part] if src is not bf and at != 0 else src.at[th, part]
+            to_mates(pick, hf.at[at, :, here], f_s.at[0], f_r.at[0])
+        hf[0, :, here] = fa[0, h, mine]
+        hf[1, :, here] = fa[3, h, mine]
+        hf[2, :, here] = fa[4, h, mine]
+        hf[3, :, here] = bf[h, mine]
+
+    def sums_start(s, j):
+        here = rows_of(q)
+        to_mates(lambda th, part: xs.at[s, th, part], hc.at[j, :, here], c_s.at[0], c_r.at[j])
+        hc[j, :, here] = xs[s, h, mine]
+
+    def all_rows(ref):
+        return ref.at[:, :, pl.ds(0, ROWS * (NQ - 1))]
+
+    def home_step(j, w):
+        if j == 0:
+            remote(all_rows(hf), all_rows(hf), f_s.at[0], f_r.at[0], other(0, 1)).wait_recv()
+        got = hc.at[j, :, pl.ds(0, ROWS * (NQ - 1))]
+        remote(got, got, c_s.at[0], c_r.at[j], other(0, 1)).wait_recv()
+        old_ref = hf if j == 0 else hcur
+        for t in range(T):
+            rate = w / (2.0 * (jnp.full((1, Y), (pe * T + t).astype(jnp.float32)) + 1.0))
+            c = hc[j, t]
+            cz = roll(c, 1, 0)
+            for i, ahead in enumerate((cz, dn_y(cz), up_y(cz), None)):
+                old = old_ref[i, t]
+                if ahead is None:
+                    new = jnp.maximum(old + 2.0 * rate * (c - 1.0), 0.0)
+                else:
+                    new = jnp.maximum(old + rate * (c - ahead), 0.0) * hm[i]
+                if j < INNER - 1:
+                    hcur[i, t] = new
+                    hacc[i, t] = new if j == 0 else hacc[i, t] + new
+                else:
+                    mean = (hacc[i, t] + new) * (1.0 / INNER)
+                    if ahead is None:
+                        bound_out[0, t] = mean
+                    else:
+                        prec_out[(0, 3, 4)[i], 0, t] = mean
 
     def out_all(what):
         dst = out_ends(what, 0, mine, pl.ds(0, ROWS * (NQ - 1)))[1]
@@ -678,6 +722,8 @@
     loads[5].wait()
     home = {k: mask_of(slope_own[...], k, depth, None) for k in (0, 3, 4)}
     loads[4].wait()
+    for i, k in enumerate((0, 3, 4)):
+        hm[i] = home[k]
     for t in range(T):
         p0, p3, p4 = (praw[k, t] * home[k] for k in (0, 3, 4))
         gh[t] = ((p0 + p3) + (p4 + braw[t])) - roll(p0 + (up_y(p3) + dn_y(p4)), -1, 0)
@@ -792,7 +838,7 @@
             edge = jnp.broadcast_to(hnr[d, t // T, pl.ds(t % T, 1)], (ROWS, Y))
             fn[d, t] = jnp.where(low, edge, roll(nraw[d, t // T, t % T], -1, 0)) * nact[d]
 
-    def settle(first, cur, acc, at, j, new, old):
+    def settle(first, cur, acc, at, j, new, old, keep=True):
         if j == 0:
             cur[at] = new
             return None
@@ -802,7 +848,8 @@
             return None
         mean = (acc[at] + new) * (1.0 / INNER)
         diff = mean - first[at]
-        first[at] = mean
+        if keep:
+            first[at] = mean
         return jnp.sum(diff * diff, axis=0)
 
     def rows_under(edge, lo, size):
@@ -912,6 +959,8 @@
             pl.when(up[0])(z_copy(0, s).start)
             for d in range(2):
                 pl.when(has[d] & up[0])(d_copy(d, 0, s).start)
+        if s >= STEPS - INNER:
+            sums_start(s, j)
         if s == 0:
             send_all(6)
             loads[2].wait()
@@ -924,7 +973,7 @@
         def arc(k, hh_, at, diff, move):
             old = p_src[k, hh_, at]
             new = jnp.maximum(old + rp[at] * diff, 0.0) * act[k, hh_][None]
-            moved = settle(fa, ca, sa, (k, hh_, at), j, new, old)
+            moved = settle(fa, ca, sa, (k, hh_, at), j, new, old, not final or k in (1, 2))
             return move if moved is None else move + moved
 
         for hh_ in range(2):
@@ -940,10 +989,11 @@
                 else:
                     mean = (bs[hh_, at] + new) * (1.0 / INNER)
                     diff = mean - bf[hh_, at]
-                    bf[hh_, at] = mean
+                    if not final:
+                        bf[hh_, at] = mean
                     move_d = move_d + jnp.sum(diff * diff, axis=0)
-        if final:
-            out_start(1)
+        if s > STEPS - INNER:
+            home_step(j - 1, w)
         wait_recv(up[0], z_copy(1, s))
 
         def own_arcs(move):
@@ -965,8 +1015,6 @@
             cz = [from_above(c[hh_], lines(zh, lo, size, s, hh_)) for hh_ in range(2)]
             move_d = arc(1, 0, at, c[0] - cz[1], move_d)
             move_d = arc(2, 1, at, c[1] - cz[0], move_d)
-        if final:
-            out_start(2)
         for d in range(2):
             wait_recv(has[d], x_copy(1 - d, s))
             wait_recv(has[d] & up[0], d_copy(1 - d, 1, s))
@@ -980,9 +1028,11 @@
             mp = jnp.sum(move_p, axis=0, keepdims=True)
             md = jnp.sum(move_d, axis=0, keepdims=True)
             reduce_start(STEPS + cyc, as_lanes(jnp.where(rows == 0, mp, jnp.where(rows == 1, md, 0.0))))
+        if s == STEPS - INNER - 1:
+            home_start()
         if final:
-            out_start(3)
-            out_start(4)
+            out_start(1)
+            home_step(j, w)
         else:
             wait_recv(up[1], z_copy(0, s))
             for d in range(2):
@@ -1039,13 +1089,14 @@
                 set_rates(w)
     few_out[T] = w[0]
     u_out[0, :, rows_of(q)] = uf[h, mine]
-    bound_out[0, :, rows_of(q)] = bf[h, mine]
-    for k in range(5):
+    for k in (1, 2):
         prec_out[k, 0, :, rows_of(q)] = fa[k, h, mine]
-    for what in range(5):
+    for what in range(2):
         out_all(what).wait_recv()
-    for what in range(5):
+    for what in range(2):
         out_all(what).wait_send()
+    remote(all_rows(hf), all_rows(hf), f_s.at[0], f_r.at[0], other(0, 1)).wait_send()
+    remote(all_rows(hc), all_rows(hc), c_s.at[0], c_r.at[0], other(0, 1)).wait_send()
     for what in range(8):
         in_all(what).wait_send()
     rest = rb.at[:, pl.ds(0, ND - 1)]
@@ -1111,6 +1162,7 @@
         scratch_shapes=[
             pltpu.VMEM((1, Y), jnp.int32), pltpu.SMEM(cap.shape, f32), pltpu.SMEM(cap.shape, f32),
             pltpu.SMEM(dens.shape, f32), pltpu.SMEM(om.shape, f32), V(1), V(NQ, 1),
+            V(3, Z), V(4, T, Z), V(4, T, Z), V(4, T, Z), V(INNER, T, Z),
             V(5, T, Z), V(T, Z), V(T, Z), V(NQ, 5, T), unit(), unit(), unit(), unit(5), V(NQ, 5, T), V(2, NPD, T, ROWS), V(2, NPD, T),
             V(2, ROWS), pltpu.VMEM((2, ROWS, Y), jnp.int32), pltpu.VMEM((4, 1, Y), jnp.int32),
             whole(5, 2), whole(5, 2), whole(5, 2), whole(2), whole(2), whole(2),
@@ -1121,7 +1173,7 @@
             edge(STEPS, 2), edge(STEPS, 2), V(slots, 1), V(slots, ND, 1),
             pltpu.SemaphoreType.REGULAR((1,)), dma((12,)), dma((8,)), dma((8,)), dma((3,)), dma((3,)), dma((2,)), dma((2,)), dma((2, 2)), dma((2, 2)),
             dma((2,)), dma((2, 2)), dma((2,)), dma((2, 2)), dma((2, 2)), dma((2, 2, 2)), dma((1,)), dma((3,)),
-            dma((5,)), dma((5,)),
+            dma((2,)), dma((2,)), dma((1,)), dma((1,)), dma((1,)), dma((INNER,)),
         ],
         compiler_params=pltpu.CompilerParams(collective_id=1, has_side_effects=True),
     )(u, prec, bound, cap, capacity, bv, tc, dens, slope, om)

time: 61.3 us -> 58 us (0.946)
  Pallas kernels: 59.9 us -> 56.6 us
    pallas_call x1, Pallas kernels: 58.4 us -> 55.1 us  [pair_call(): pl.pallas_call(functools.partial(pair_kernel, NS, NPD, T, Z, Y), out_shap...]
where the time goes in v6:
time: 58 us; the launch traced here: 57.8 us
  Pallas kernels  56.6 us (98%)
  between operations  1.29 us (2%)
    pallas_call x1, Pallas kernels, pair_call(): pl.pallas_call(functools.partial(pair_kernel, NS, NPD, T, Z, Y), out_shap...  55.1 us
    pallas_call x1, Pallas kernels, pair_call(): pl.pallas_call(store_kernel, out_shape=(jax.ShapeDtypeStruct(u.shape, f32...  1.47 us

profile of v6, /device:TPU:0, one launch (start us, length us, event | category | flops | bytes accessed | tf_op | source)
XLA Modules:
  0.0 57.8 jit_solution(1050791435814534484)
XLA Ops:
  1.3 55.1 %shard_map.137 = (f32[1,4,64,128]{3,2,1,0:T(8,128)S(1)}, f32[5,1,4,64,128]{4,3,2,1,0:T(8,128)S(1)}, f32[1,4,64,128]{3,2,1,0:T(8,128)S(1)}, f32[5,128]{1,0:T(8,128)S(1)}) custom-call(f32[1,4,64,128]{3,2,1,0:T(8,128)} %u_ref.1, f32[5,1,4,64,128]{4,3,2,1,0:T(8,128)} %prec_ref.1, f32[1,4,64,128]{3,2,1,0:T(8,128)} %bound_ref.1, f32[4]{0:T(128)} %cap_ref.1, ...), custom_call_target="tpu_custom_call" | custom-call | tf_op jit(solution)/shard_map/pallas_call | solution.py:1152
  56.4 1.5 %shard_map.138 = (f32[1,4,64,128]{3,2,1,0:T(8,128)}, f32[5,1,4,64,128]{4,3,2,1,0:T(8,128)}, f32[1,4,64,128]{3,2,1,0:T(8,128)}, f32[4]{0:T(128)}, f32[1]{0:T(128)}) custom-call(f32[1,4,64,128]{3,2,1,0:T(8,128)S(1)} %get-tuple-element.9.u_ref, f32[5,1,4,64,128]{4,3,2,1,0:T(8,128)S(1)} %get-tuple-element.10.prec_ref, ...), custom_call_target="tpu_custom_call" | custom-call | tf_op jit(solution)/shard_map/pallas_call | solution.py:1180

commit v7 on v6

--- a/solution.py
+++ b/solution.py
@@ -16,7 +16,7 @@
 SLOPE = 11.0
 MESH = pl.DeviceIdType.MESH
 ROWS = 8
-CHUNK = 8
+CHUNK = 4
 
 
 def kernel(
@@ -948,8 +948,6 @@
             row = jnp.where(rows == t, jnp.sum(mined, axis=0, keepdims=True), row)
         if not last:
             reduce_start(s, totals(row, s))
-        if final:
-            out_start(0)
         pl.when(up[1])(z_copy(1, s).start)
         for d in range(2):
             pl.when(has[d])(x_copy(d, s).start)
@@ -959,6 +957,8 @@
             pl.when(up[0])(z_copy(0, s).start)
             for d in range(2):
                 pl.when(has[d] & up[0])(d_copy(d, 0, s).start)
+        if final:
+            out_start(0)
         if s >= STEPS - INNER:
             sums_start(s, j)
         if s == 0:

time: 58 us -> 57.9 us (level)
  no operation moved by 1% of the time
where the time goes in v7:
time: 57.9 us; the launch traced here: 57.8 us
  Pallas kernels  56.5 us (98%)
  between operations  1.29 us (2%)
    pallas_call x1, Pallas kernels, pair_call(): pl.pallas_call(functools.partial(pair_kernel, NS, NPD, T, Z, Y), out_shap...  55 us
    pallas_call x1, Pallas kernels, pair_call(): pl.pallas_call(store_kernel, out_shape=(jax.ShapeDtypeStruct(u.shape, f32...  1.47 us

profile of v7, /device:TPU:0, one launch (start us, length us, event | category | flops | bytes accessed | tf_op | source)
XLA Modules:
  0.0 57.8 jit_solution(3415297777548871220)
XLA Ops:
  1.3 55.0 %shard_map.137 = (f32[1,4,64,128]{3,2,1,0:T(8,128)S(1)}, f32[5,1,4,64,128]{4,3,2,1,0:T(8,128)S(1)}, f32[1,4,64,128]{3,2,1,0:T(8,128)S(1)}, f32[5,128]{1,0:T(8,128)S(1)}) custom-call(f32[1,4,64,128]{3,2,1,0:T(8,128)} %u_ref.1, f32[5,1,4,64,128]{4,3,2,1,0:T(8,128)} %prec_ref.1, f32[1,4,64,128]{3,2,1,0:T(8,128)} %bound_ref.1, f32[4]{0:T(128)} %cap_ref.1, ...), custom_call_target="tpu_custom_call" | custom-call | tf_op jit(solution)/shard_map/pallas_call | solution.py:1152
  56.3 1.5 %shard_map.138 = (f32[1,4,64,128]{3,2,1,0:T(8,128)}, f32[5,1,4,64,128]{4,3,2,1,0:T(8,128)}, f32[1,4,64,128]{3,2,1,0:T(8,128)}, f32[4]{0:T(128)}, f32[1]{0:T(128)}) custom-call(f32[1,4,64,128]{3,2,1,0:T(8,128)S(1)} %get-tuple-element.9.u_ref, f32[5,1,4,64,128]{4,3,2,1,0:T(8,128)S(1)} %get-tuple-element.10.prec_ref, ...), custom_call_target="tpu_custom_call" | custom-call | tf_op jit(solution)/shard_map/pallas_call | solution.py:1180
